TPU v7x, 32 devices: a whole 2x2x4 slice. The times are simulated.
32 devices in a mesh: seq: 8 (over z, x), fsdp: 4 (over y, core).
Axes of the slice: x: 2, y: 2, z: 4, core: 2. Of those that a mesh axis runs over, the one named last changes fastest.
Arguments:
- tokens: bfloat16 [8192, 1024], P(('seq', 'fsdp')), may hold values from -6 to 6
- attn_gain: bfloat16 [1024], P(('seq', 'fsdp')), may hold values from 0.25 to 1.75
- w_query: bfloat16 [1024, 1024], P(('seq', 'fsdp')), may hold values from -0.1875 to 0.1875
- w_key: bfloat16 [1024, 1024], P(('seq', 'fsdp')), may hold values from -0.1875 to 0.1875
- w_value: bfloat16 [1024, 1024], P(('seq', 'fsdp')), may hold values from -0.1875 to 0.1875
- conv_weight: bfloat16 [4, 3072], P(None, ('seq', 'fsdp')), may hold values from -3 to 3
- w_beta: bfloat16 [1024, 8], P(('seq', 'fsdp')), may hold values from -0.1875 to 0.1875
- w_gate_out: bfloat16 [1024, 1024], P(('seq', 'fsdp')), may hold values from -0.1875 to 0.1875
- onorm_gain: bfloat16 [128], P(('seq', 'fsdp')), may hold values from 0.25 to 1.75
- w_out: bfloat16 [1024, 1024], P(('seq', 'fsdp')), may hold values from -0.375 to 0.375
- mlp_gain: bfloat16 [1024], P(('seq', 'fsdp')), may hold values from 0.25 to 1.75
- w_mlp_gate: bfloat16 [1024, 2816], P(('seq', 'fsdp')), may hold values from -0.1875 to 0.1875
- w_mlp_up: bfloat16 [1024, 2816], P(('seq', 'fsdp')), may hold values from -0.1875 to 0.1875
- w_down: bfloat16 [2816, 1024], P(('seq', 'fsdp')), may hold values from -0.21875 to 0.21875
- seq_lengths: int32 [4], replicated, may hold values from 1024 to 4096, as said below
- cotangent: bfloat16 [8192, 1024], P(('seq', 'fsdp')), may hold values from -6 to 6
Outputs:
- output: bfloat16 [8192, 1024], P(('seq', 'fsdp'))
- grad_tokens: float32 [8192, 1024], P(('seq', 'fsdp'))
- grad_attn_gain: float32 [1024], P(('seq', 'fsdp'))
- grad_query: float32 [1024, 1024], P(('seq', 'fsdp'))
- grad_key: float32 [1024, 1024], P(('seq', 'fsdp'))
- grad_value: float32 [1024, 1024], P(('seq', 'fsdp'))
- grad_conv: float32 [4, 3072], P(None, ('seq', 'fsdp'))
- grad_beta: float32 [1024, 8], P(('seq', 'fsdp'))
- grad_gate_out: float32 [1024, 1024], P(('seq', 'fsdp'))
- grad_onorm: float32 [128], P(('seq', 'fsdp'))
- grad_out: float32 [1024, 1024], P(('seq', 'fsdp'))
- grad_mlp_gain: float32 [1024], P(('seq', 'fsdp'))
- grad_mlp_gate: float32 [1024, 2816], P(('seq', 'fsdp'))
- grad_mlp_up: float32 [1024, 2816], P(('seq', 'fsdp'))
- grad_down: float32 [2816, 1024], P(('seq', 'fsdp'))
Inputs may be any that keep to these rules, and one draw needn't show every extreme that they name: `seq_lengths`: every length is a multiple of 64; the lengths sum to 8192; one sequence has exactly 4096 tokens and two have exactly 1024 tokens each.
All inputs are finite; a program needn't handle non-finite values.
Results may differ from a plain program's by a relative error of at most 0.013.
The roundings to bfloat16 on the way count: a program that leaves them out, or rounds other values in their place, can miss the bound.
Values may be sent and summed in bfloat16 or wider, within the bound.
No kernel may reach another device: no remote copies, remote signals or barrier semaphores. Data moves between devices by JAX's collectives and lax.ppermute only.
A program may use at most 448 MiB of HBM per device.

v0:
```python
from functools import partial

import jax
import jax.numpy as jnp
from jax import lax
from jax.sharding import PartitionSpec as P

CONV = 4
BLOCK = 64


highest = lax.Precision.HIGHEST


def passed_along(array, axis, by):
    size = lax.axis_size(axis)
    pairs = [(i, i + by) for i in range(size) if 0 <= i + by < size]
    return lax.ppermute(array, axis, pairs)


def entering_2(array, axis, combine, identity):
    size, index = (lax.axis_size(axis), lax.axis_index(axis))
    everything = jax.tree.map(lambda part: lax.all_gather(part, axis), array)
    start = jax.tree.map(
        lambda part, zero: jnp.broadcast_to(jnp.asarray(zero, part.dtype), part.shape),
        array,
        identity,
    )

    def hop(k, before):
        reached = k < index
        new = combine(before, jax.tree.map(lambda part: part[k], everything))
        return jax.tree.map(lambda a, b: jnp.where(reached, a, b), new, before)

    return lax.fori_loop(0, size, hop, start)


def entering_3(array, axis, join, neutral):
    count = lax.axis_size(axis)
    place = lax.axis_index(axis)
    ahead = count - 1 - place
    gathered = jax.tree.map(
        lambda a, kind: lax.all_gather(a.astype(kind), axis),
        array,
        jax.tree.map(lambda a: jnp.bfloat16 if a.dtype == jnp.float32 else a.dtype, array),
    )
    state = jax.tree.map(lambda a, e: jnp.zeros_like(a) + jnp.asarray(e, a.dtype), array, neutral)

    def one(hop, state):
        source = count - 1 - hop
        return join(
            state,
            jax.tree.map(
                lambda a, own: lax.dynamic_index_in_dim(a, source, 0, False).astype(own.dtype),
                gathered,
                array,
            ),
        )

    return lax.fori_loop(0, ahead, one, state)


def rms_scale(values, gain):
    return values * lax.rsqrt(jnp.mean(values * values, axis=-1, keepdims=True) + 1e-05) * gain


def unit_rows(values):
    return values * lax.rsqrt(jnp.sum(values * values, axis=-1, keepdims=True) + 1e-06)


def swiglu(gate_rows, up_rows):
    return jax.nn.silu(gate_rows) * up_rows


def seq_offsets(seq_lengths, positions):
    starts = jnp.cumsum(seq_lengths) - seq_lengths
    begins = jnp.max(jnp.where(starts[None, :] <= positions[:, None], starts[None, :], 0), axis=1)
    return positions - begins


def conv_front(extended, conv_rows, beta_logit, distance, head_count):
    row_count = distance.shape[0]
    summed = conv_rows[CONV - 1] * extended[CONV - 1 :]
    for offset in range(CONV - 1):
        lagged = CONV - 1 - offset
        inside = (distance >= lagged).astype(jnp.float32)[:, None]
        summed = summed + conv_rows[offset] * extended[offset : offset + row_count] * inside
    active = jax.nn.silu(summed).reshape(row_count, 3, head_count, -1)
    return (
        unit_rows(active[:, 0]),
        unit_rows(active[:, 1]),
        active[:, 2],
        jax.nn.sigmoid(beta_logit),
    )


def blocked(array):
    row_count = array.shape[0]
    return jnp.swapaxes(array.reshape((row_count // BLOCK, BLOCK) + array.shape[1:]), 1, 2)


def wy_terms(key_rows, values, beta_rows):
    key_blocks = blocked(key_rows)
    value_blocks = blocked(values)
    beta_blocks = blocked(beta_rows)
    intersections = jnp.einsum("nhck,nhdk->nhcd", key_blocks, key_blocks, precision=highest)
    strict = jnp.tril(jnp.ones((BLOCK, BLOCK), jnp.float32), -1)
    nilpotent = -(intersections * beta_blocks[..., :, None] * strict)
    inverse = jnp.eye(BLOCK, dtype=jnp.float32) + nilpotent
    covered = 2
    while covered < BLOCK:
        nilpotent = jnp.einsum("nhcd,nhde->nhce", nilpotent, nilpotent, precision=highest)
        inverse = inverse + jnp.einsum("nhcd,nhde->nhce", inverse, nilpotent, precision=highest)
        covered = covered * 2
    w_rows = jnp.einsum(
        "nhcd,nhdk->nhck", inverse, key_blocks * beta_blocks[..., None], precision=highest
    )
    u_rows = jnp.einsum(
        "nhcd,nhdk->nhck", inverse, value_blocks * beta_blocks[..., None], precision=highest
    )
    return (w_rows, u_rows)


def block_summary(key_rows, w_rows, u_rows, restarts):
    key_blocks = blocked(key_rows)
    head_size = key_blocks.shape[-1]
    identity_block = jnp.eye(head_size, dtype=jnp.float32)
    decays = identity_block - jnp.einsum("nhck,nhcd->nhkd", w_rows, key_blocks, precision=highest)
    pushes = jnp.einsum("nhcv,nhck->nhvk", u_rows, key_blocks, precision=highest)

    def compose(carried, inputs):
        linear, constant = carried
        decay_block, push_block, restart = inputs
        linear = (1.0 - restart) * jnp.einsum(
            "hij,hjk->hik", linear, decay_block, precision=highest
        )
        constant = (1.0 - restart) * jnp.einsum(
            "hij,hjk->hik", constant, decay_block, precision=highest
        ) + push_block
        return ((linear, constant), None)

    start_pair = (
        jnp.broadcast_to(identity_block, decays.shape[1:]),
        jnp.zeros(pushes.shape[1:], jnp.float32),
    )
    summary, unused = lax.scan(compose, start_pair, (decays, pushes, restarts))
    return summary


def block_pass(queries, key_rows, w_rows, u_rows, entering, restarts):
    query_blocks = blocked(queries)
    key_blocks = blocked(key_rows)
    causal = jnp.tril(jnp.ones((BLOCK, BLOCK), jnp.float32))

    def advance(carried, inputs):
        query_part, key_part, w_part, u_part, restart = inputs
        initial = carried * (1.0 - restart)
        corrected = u_part - jnp.einsum("hck,hvk->hcv", w_part, initial, precision=highest)
        scores = jnp.einsum("hck,hdk->hcd", query_part, key_part, precision=highest) * causal
        result = jnp.einsum("hck,hvk->hcv", query_part, initial, precision=highest) + jnp.einsum(
            "hcd,hdv->hcv", scores, corrected, precision=highest
        )
        leaving = initial + jnp.einsum("hcv,hck->hvk", corrected, key_part, precision=highest)
        return (leaving, result)

    leaving, results = lax.scan(
        advance, entering, (query_blocks, key_blocks, w_rows, u_rows, restarts)
    )
    return (jnp.swapaxes(results, 1, 2).reshape(queries.shape), leaving)


def chain_join(earlier, later):
    return (
        jnp.einsum("hij,hjk->hik", earlier[0], later[0], precision=highest),
        jnp.einsum("hij,hjk->hik", earlier[1], later[0], precision=highest) + later[1],
    )


def output_gate(mixed_heads, gate_logit, onorm_scale):
    normalized = (
        mixed_heads
        * lax.rsqrt(jnp.mean(mixed_heads * mixed_heads, axis=-1, keepdims=True) + 1e-05)
        * onorm_scale
    )
    return (normalized * jax.nn.silu(gate_logit.reshape(mixed_heads.shape))).reshape(
        gate_logit.shape
    )


def local(
    tokens,
    attn_gain,
    w_query,
    w_key,
    w_value,
    conv_weight,
    w_beta,
    w_gate_out,
    onorm_gain,
    w_out,
    mlp_gain,
    w_mlp_gate,
    w_mlp_up,
    w_down,
    seq_lengths,
    cotangent,
):
    row_count = tokens.shape[0]
    positions = lax.axis_index(("seq", "fsdp")) * row_count + jnp.arange(row_count, dtype=jnp.int32)
    distance = seq_offsets(seq_lengths, positions)
    restarts = (distance[::BLOCK] == 0).astype(jnp.float32)
    attn_set = (
        lax.all_gather(attn_gain, ("seq", "fsdp"), axis=0, tiled=True),
        lax.all_gather(w_query, ("seq", "fsdp"), axis=0, tiled=True),
        lax.all_gather(w_key, ("seq", "fsdp"), axis=0, tiled=True),
        lax.all_gather(w_value, ("seq", "fsdp"), axis=0, tiled=True),
        lax.all_gather(conv_weight, ("seq", "fsdp"), axis=1, tiled=True),
        lax.all_gather(w_beta, ("seq", "fsdp"), axis=0, tiled=True),
        lax.all_gather(w_gate_out, ("seq", "fsdp"), axis=0, tiled=True),
        lax.all_gather(onorm_gain, ("seq", "fsdp"), axis=0, tiled=True),
        lax.all_gather(w_out, ("seq", "fsdp"), axis=0, tiled=True),
    )
    (
        full_gain,
        full_query,
        full_key,
        full_value,
        full_conv,
        full_beta,
        full_gate_out,
        full_onorm,
        full_out,
    ) = attn_set
    model_width = full_query.shape[0]
    head_count = full_beta.shape[1]
    token_rows = tokens.astype(jnp.float32)
    normed32, norm_one_back = jax.vjp(rms_scale, token_rows, full_gain.astype(jnp.float32))
    normed = normed32.astype(jnp.bfloat16)
    projected = jnp.concatenate(
        [
            jnp.dot(normed, full_query, preferred_element_type=jnp.float32),
            jnp.dot(normed, full_key, preferred_element_type=jnp.float32),
            jnp.dot(normed, full_value, preferred_element_type=jnp.float32),
        ],
        axis=1,
    ).astype(jnp.bfloat16)
    rim_rows = passed_along(projected[row_count - (CONV - 1) :], ("seq", "fsdp"), 1)
    extended = jnp.concatenate([rim_rows, projected], axis=0).astype(jnp.float32)
    beta_logit = jnp.dot(normed, full_beta, preferred_element_type=jnp.float32)
    gate_logit = jnp.dot(normed, full_gate_out, preferred_element_type=jnp.float32)
    front = partial(conv_front, distance=distance, head_count=head_count)
    front_out, front_back = jax.vjp(front, extended, full_conv.astype(jnp.float32), beta_logit)
    queries, key_rows, values, beta_rows = front_out
    wy_out, wy_back = jax.vjp(wy_terms, key_rows, values, beta_rows)
    w_rows, u_rows = wy_out
    linear, constant = block_summary(key_rows, w_rows, u_rows, restarts)
    identity_pair = (
        jnp.broadcast_to(jnp.eye(linear.shape[-1], dtype=jnp.float32), linear.shape),
        jnp.zeros(constant.shape, jnp.float32),
    )
    prefix = entering_2((linear, constant), ("seq", "fsdp"), chain_join, identity_pair)
    entering = prefix[1]
    passing = partial(block_pass, restarts=restarts)
    pass_out, pass_back = jax.vjp(passing, queries, key_rows, w_rows, u_rows, entering)
    mixed_heads = pass_out[0]
    branch32, gate_back = jax.vjp(
        output_gate, mixed_heads, gate_logit, full_onorm.astype(jnp.float32)
    )
    branch = branch32.astype(jnp.bfloat16)
    hidden = token_rows + jnp.dot(branch, full_out, preferred_element_type=jnp.float32)
    mlp_set = (
        lax.all_gather(mlp_gain, ("seq", "fsdp"), axis=0, tiled=True),
        lax.all_gather(w_mlp_gate, ("seq", "fsdp"), axis=0, tiled=True),
        lax.all_gather(w_mlp_up, ("seq", "fsdp"), axis=0, tiled=True),
        lax.all_gather(w_down, ("seq", "fsdp"), axis=0, tiled=True),
    )
    full_mlp_gain, full_mlp_gate, full_mlp_up, full_down = mlp_set
    normed_two32, norm_two_back = jax.vjp(rms_scale, hidden, full_mlp_gain.astype(jnp.float32))
    normed_two = normed_two32.astype(jnp.bfloat16)
    gate_rows = jnp.dot(normed_two, full_mlp_gate, preferred_element_type=jnp.float32)
    up_rows = jnp.dot(normed_two, full_mlp_up, preferred_element_type=jnp.float32)
    inner32, inner_back = jax.vjp(swiglu, gate_rows, up_rows)
    inner_act = inner32.astype(jnp.bfloat16)
    output = (hidden + jnp.dot(inner_act, full_down, preferred_element_type=jnp.float32)).astype(
        jnp.bfloat16
    )
    back_mlp_gate, back_mlp_up, back_down = (
        lax.all_gather(w_mlp_gate, ("seq", "fsdp"), axis=0, tiled=True),
        lax.all_gather(w_mlp_up, ("seq", "fsdp"), axis=0, tiled=True),
        lax.all_gather(w_down, ("seq", "fsdp"), axis=0, tiled=True),
    )
    d_inner = jnp.dot(cotangent, back_down.T, preferred_element_type=jnp.float32)
    grad_down_term = jnp.dot(inner_act.T, cotangent, preferred_element_type=jnp.float32)
    d_gate32, d_up32 = inner_back(d_inner)
    d_gate = d_gate32.astype(jnp.bfloat16)
    d_up = d_up32.astype(jnp.bfloat16)
    grad_mlp_gate_term = jnp.dot(normed_two.T, d_gate, preferred_element_type=jnp.float32)
    grad_mlp_up_term = jnp.dot(normed_two.T, d_up, preferred_element_type=jnp.float32)
    d_normed_two = jnp.dot(d_gate, back_mlp_gate.T, preferred_element_type=jnp.float32) + jnp.dot(
        d_up, back_mlp_up.T, preferred_element_type=jnp.float32
    )
    d_hidden_norm, grad_mlp_gain_term = norm_two_back(d_normed_two)
    d_hidden = cotangent.astype(jnp.float32) + d_hidden_norm
    mlp_terms = (grad_mlp_gain_term, grad_mlp_gate_term, grad_mlp_up_term, grad_down_term)
    mlp_grads = (
        lax.psum_scatter(mlp_terms[0], ("seq", "fsdp"), scatter_dimension=0, tiled=True),
        lax.psum_scatter(mlp_terms[1], ("seq", "fsdp"), scatter_dimension=0, tiled=True),
        lax.psum_scatter(mlp_terms[2], ("seq", "fsdp"), scatter_dimension=0, tiled=True),
        lax.psum_scatter(mlp_terms[3], ("seq", "fsdp"), scatter_dimension=0, tiled=True),
    )
    back_query, back_key, back_value, back_beta, back_gate_out, back_out = (
        lax.all_gather(w_query, ("seq", "fsdp"), axis=0, tiled=True),
        lax.all_gather(w_key, ("seq", "fsdp"), axis=0, tiled=True),
        lax.all_gather(w_value, ("seq", "fsdp"), axis=0, tiled=True),
        lax.all_gather(w_beta, ("seq", "fsdp"), axis=0, tiled=True),
        lax.all_gather(w_gate_out, ("seq", "fsdp"), axis=0, tiled=True),
        lax.all_gather(w_out, ("seq", "fsdp"), axis=0, tiled=True),
    )
    d_attn = d_hidden.astype(jnp.bfloat16)
    grad_out_term = jnp.dot(branch.T, d_attn, preferred_element_type=jnp.float32)
    d_branch = jnp.dot(d_attn, back_out.T, preferred_element_type=jnp.float32)
    d_mixed, d_gate_logit32, grad_onorm_term = gate_back(d_branch)
    d_gate_logit = d_gate_logit32.astype(jnp.bfloat16)
    first_grads = pass_back((d_mixed, jnp.zeros_like(entering)))
    suffix = entering_3(
        (jnp.swapaxes(linear, 1, 2), first_grads[4]), ("seq", "fsdp"), chain_join, identity_pair
    )
    second_grads = pass_back((jnp.zeros_like(mixed_heads), suffix[1]))
    d_queries = first_grads[0] + second_grads[0]
    d_keys_pass = first_grads[1] + second_grads[1]
    d_w_rows = first_grads[2] + second_grads[2]
    d_u_rows = first_grads[3] + second_grads[3]
    d_keys_wy, d_values, d_betas = wy_back((d_w_rows, d_u_rows))
    d_extended, grad_conv_term, d_beta32 = front_back(
        (d_queries, d_keys_pass + d_keys_wy, d_values, d_betas)
    )
    d_beta_logit = d_beta32.astype(jnp.bfloat16)
    rim_back = passed_along(
        d_extended[: CONV - 1].astype(jnp.bfloat16), ("seq", "fsdp"), -1
    ).astype(jnp.float32)
    d_local = d_extended[CONV - 1 :]
    d_projected = jnp.concatenate(
        [d_local[: row_count - (CONV - 1)], d_local[row_count - (CONV - 1) :] + rim_back], axis=0
    ).astype(jnp.bfloat16)
    d_query_cols = d_projected[:, :model_width]
    d_key_cols = d_projected[:, model_width : 2 * model_width]
    d_value_cols = d_projected[:, 2 * model_width :]
    grad_query_term = jnp.dot(normed.T, d_query_cols, preferred_element_type=jnp.float32)
    grad_key_term = jnp.dot(normed.T, d_key_cols, preferred_element_type=jnp.float32)
    grad_value_term = jnp.dot(normed.T, d_value_cols, preferred_element_type=jnp.float32)
    grad_beta_term = jnp.dot(normed.T, d_beta_logit, preferred_element_type=jnp.float32)
    grad_gate_out_term = jnp.dot(normed.T, d_gate_logit, preferred_element_type=jnp.float32)
    d_normed = (
        jnp.dot(d_query_cols, back_query.T, preferred_element_type=jnp.float32)
        + jnp.dot(d_key_cols, back_key.T, preferred_element_type=jnp.float32)
        + jnp.dot(d_value_cols, back_value.T, preferred_element_type=jnp.float32)
        + jnp.dot(d_beta_logit, back_beta.T, preferred_element_type=jnp.float32)
        + jnp.dot(d_gate_logit, back_gate_out.T, preferred_element_type=jnp.float32)
    )
    d_token_norm, grad_attn_gain_term = norm_one_back(d_normed)
    grad_tokens = d_hidden + d_token_norm
    attn_terms = (
        grad_attn_gain_term,
        grad_query_term,
        grad_key_term,
        grad_value_term,
        grad_conv_term,
        grad_beta_term,
        grad_gate_out_term,
        grad_onorm_term,
        grad_out_term,
    )
    attn_grads = (
        lax.psum_scatter(attn_terms[0], ("seq", "fsdp"), scatter_dimension=0, tiled=True),
        lax.psum_scatter(attn_terms[1], ("seq", "fsdp"), scatter_dimension=0, tiled=True),
        lax.psum_scatter(attn_terms[2], ("seq", "fsdp"), scatter_dimension=0, tiled=True),
        lax.psum_scatter(attn_terms[3], ("seq", "fsdp"), scatter_dimension=0, tiled=True),
        lax.psum_scatter(attn_terms[4], ("seq", "fsdp"), scatter_dimension=1, tiled=True),
        lax.psum_scatter(attn_terms[5], ("seq", "fsdp"), scatter_dimension=0, tiled=True),
        lax.psum_scatter(attn_terms[6], ("seq", "fsdp"), scatter_dimension=0, tiled=True),
        lax.psum_scatter(attn_terms[7], ("seq", "fsdp"), scatter_dimension=0, tiled=True),
        lax.psum_scatter(attn_terms[8], ("seq", "fsdp"), scatter_dimension=0, tiled=True),
    )
    return (
        output,
        grad_tokens,
        attn_grads[0],
        attn_grads[1],
        attn_grads[2],
        attn_grads[3],
        attn_grads[4],
        attn_grads[5],
        attn_grads[6],
        attn_grads[7],
        attn_grads[8],
        mlp_grads[0],
        mlp_grads[1],
        mlp_grads[2],
        mlp_grads[3],
    )


def solution(mesh):
    return jax.shard_map(
        local,
        mesh=mesh,
        in_specs=(
            P(("seq", "fsdp"), None),
            P(("seq", "fsdp")),
            P(("seq", "fsdp"), None),
            P(("seq", "fsdp"), None),
            P(("seq", "fsdp"), None),
            P(None, ("seq", "fsdp")),
            P(("seq", "fsdp"), None),
            P(("seq", "fsdp"), None),
            P(("seq", "fsdp")),
            P(("seq", "fsdp"), None),
            P(("seq", "fsdp")),
            P(("seq", "fsdp"), None),
            P(("seq", "fsdp"), None),
            P(("seq", "fsdp"), None),
            P(),
            P(("seq", "fsdp"), None),
        ),
        out_specs=(
            P(("seq", "fsdp"), None),
            P(("seq", "fsdp"), None),
            P(("seq", "fsdp")),
            P(("seq", "fsdp"), None),
            P(("seq", "fsdp"), None),
            P(("seq", "fsdp"), None),
            P(None, ("seq", "fsdp")),
            P(("seq", "fsdp"), None),
            P(("seq", "fsdp"), None),
            P(("seq", "fsdp")),
            P(("seq", "fsdp"), None),
            P(("seq", "fsdp")),
            P(("seq", "fsdp"), None),
            P(("seq", "fsdp"), None),
            P(("seq", "fsdp"), None),
        ),
        check_vma=False,
    )
```

profile of v0, /device:TPU:0, one launch (start us, length us, event | category | flops | bytes accessed | tf_op | source)
XLA Modules:
  0.0 2583.7 jit_solution(2421566339869992266)
XLA Ops:
  12.0 42.2 %all-reduce.18 = (bf16[1024]{0:T(1024)(128)(2,1)S(1)}, bf16[128]{0:T(256)(128)(2,1)S(1)}, bf16[1024]{0:T(1024)(128)(2,1)S(1)}) all-reduce(bf16[1024]{0:T(1024)(128)(2,1)S(1)} %dynamic-update-slice, bf16[128]{0:T(256)(128)(2,1)S(1)} %dynamic-update-slice.1, ...), channel_id=1, replica_groups=mesh['seq'=8,'fsdp'=4] {'seq','fsdp'}, use_global_device_ids=true, to_apply=%add.11 | all-reduce | flops 2176 | bytes 8704
  54.2 40.5 %all-gather.4 = bf16[32,96,4]{1,2,0:T(4,128)(2,1)S(1)} all-gather(bf16[1,96,4]{1,2,0:T(4,128)(2,1)} %bitcast.643), channel_id=1, replica_groups=mesh['seq'=8,'fsdp'=4] {'seq','fsdp'}, dimensions={0}, use_global_device_ids=true | all-gather | bytes 25344 | tf_op jit(solution)/shard_map/all_gather | solution.py:217
  94.9 37.4 %all-gather.5 = bf16[32,32,8]{1,2,0:T(8,128)(2,1)S(1)} all-gather(bf16[1,32,8]{1,2,0:T(8,128)(2,1)} %bitcast.642), channel_id=1, replica_groups=mesh['seq'=8,'fsdp'=4] {'seq','fsdp'}, dimensions={0}, use_global_device_ids=true | all-gather | bytes 16896 | tf_op jit(solution)/shard_map/all_gather | solution.py:218
  141.9 44.7 %all-gather.19.cloned.1.call-done = bf16[1024,1024]{1,0:T(8,128)(2,1)} async-done(((bf16[32,1024]{1,0:T(8,128)(2,1)}), bf16[1024,1024]{1,0:T(8,128)(2,1)}) %all-gather.19.cloned.1.call-update) | async-done | bytes 2097168 | tf_op jit(solution)/shard_map/all_gather | solution.py:214
  234.1 22.7 while.111
  265.2 109.4 %all-gather.35.cloned.1.call-done = f32[256,128,128]{2,1,0:T(8,128)} async-done(((f32[8,128,128]{2,1,0:T(8,128)}), f32[256,128,128]{2,1,0:T(8,128)}) %all-gather.35.cloned.1.call-update) | async-done | bytes 16777232 | tf_op jit(solution)/shard_map/all_gather | solution.py:23
  374.7 115.8 %all-gather.37.cloned.1.call-done = f32[256,128,128]{2,1,0:T(8,128)} async-done(((f32[8,128,128]{2,1,0:T(8,128)}), f32[256,128,128]{2,1,0:T(8,128)}) %all-gather.37.cloned.1.call-update) | async-done | bytes 16777232 | tf_op jit(solution)/shard_map/all_gather | solution.py:23
  490.5 225.0 %while.112 = (s32[]{:T(128)}, f32[8,128,128]{1,2,0:T(8,128)}, s32[]{:T(128)}, f32[32,8,128,128]{3,2,1,0:T(8,128)}, f32[32,8,128,128]{3,2,1,0:T(8,128)}, /*index=5*/s32[]{:T(128)}, s32[]{:T(128)}) while((s32[]{:T(128)}, f32[8,128,128]{1,2,0:T(8,128)}, s32[]{:T(128)}, f32[32,8,128,128]{3,2,1,0:T(8,128)}, ...), condition=%wide.region_7.8_spmd.clone, body=%wide.region_6.7_spmd.clone.sunk | while | flops 201850880 | bytes 5769315 | solution.py:35
  718.9 53.4 %while.109 = (s32[]{:T(128)}, f32[8,128,128]{2,1,0:T(8,128)S(1)}, f32[4,8,64,128]{3,2,1,0:T(8,128)}, f32[4]{0:T(128)S(1)}, f32[4,8,128,128]{3,2,1,0:T(8,128)}, /...) while((s32[]{:T(128)}, f32[8,128,128]{2,1,0:T(8,128)S(1)}, ...), condition=%wide.region_10.11_spmd.clone, body=%wide.region_9.10_spmd.clone.sunk | while | flops 403480576 | bytes 7656613 | solution.py:166
  786.0 6.0 fusion.273
  792.1 5.9 fusion.274
  797.9 15.2 all-gather.33.cloned.1.call-done
  813.2 8.4 multiply_convert_fusion
  821.5 5.6 fusion.275
  842.6 56.9 %while.113 = (s32[]{:T(128)}, f32[8,128,128]{2,1,0:T(8,128)S(1)}, f32[4,8,64,128]{3,1,2,0:T(8,128)}, f32[4,8,64,128]{3,2,1,0:T(8,128)}, f32[4,8,64,128]{3,2,1,0:...) while((s32[]{:T(128)}, f32[8,128,128]{2,1,0:T(8,128)S(1)}, ...), condition=%wide.region_16.17_spmd.clone, body=%wide.region_15.16_spmd.clone.sunk | while | flops 806461440 | bytes 28761896 | solution.py:166
  901.1 76.0 %all-gather.41.cloned.1.call-done = bf16[256,128,128]{2,1,0:T(8,128)(2,1)} async-done(((bf16[8,128,128]{2,1,0:T(8,128)(2,1)}), bf16[256,128,128]{2,1,0:T(8,128)(2,1)}) %all-gather.41.cloned.1.call-update) | async-done | bytes 8388624 | tf_op jit(solution)/shard_map/all_gather | solution.py:43
  977.1 82.1 %while.108 = (s32[]{:T(128)}, f32[8,128,128]{1,2,0:T(8,128)S(1)}, s32[]{:T(128)}, bf16[32,8,128,128]{3,2,1,0:T(8,128)(2,1)}, bf16[32,8,128,128]{3,2,1,0:T(8,128)...) while((s32[]{:T(128)}, f32[8,128,128]{1,2,0:T(8,128)S(1)}, s32[]{:T(128)}, ...), condition=%wide.region_18.19_spmd, body=%wide.region_17.18_spmd.sunk | while | flops 201588736 | bytes 3670163 | solution.py:60
  1063.9 50.5 %while.110 = (s32[]{:T(128)}, f32[8,128,128]{2,1,0:T(8,128)S(1)}, f32[4,8,64,128]{3,1,2,0:T(8,128)}, f32[4,8,64,128]{3,2,1,0:T(8,128)}, f32[4,8,64,128]{3,2,1,0:...) while((s32[]{:T(128)}, f32[8,128,128]{2,1,0:T(8,128)S(1)}, ...), condition=%wide.region_20.21_spmd.clone, body=%wide.region_19.20_spmd.clone.sunk | while | flops 806068224 | bytes 23514876 | solution.py:166
  1193.2 5.9 fusion.282
  1200.5 5.9 fusion.283
  1207.9 5.9 fusion.284
  1234.2 5.7 fusion.172
  1244.6 37.1 %all-reduce.17 = (f32[1024]{0:T(1024)S(1)}, f32[128]{0:T(128)S(1)}, f32[1024]{0:T(1024)S(1)}) all-reduce(f32[1024]{0:T(1024)S(1)} %get-tuple-element.1306, f32[128]{0:T(128)S(1)} %copy-done.100, f32[1024]{0:T(1024)S(1)} %copy-done.99), channel_id=6, replica_groups=mesh['seq'=8,'fsdp'=4] {'seq','fsdp'}, use_global_device_ids=true, to_apply=%region_28.29.clone | all-reduce | flops 2176 | bytes 17408
  1286.2 123.4 %reduce-scatter.33.cloned.1.call-done = f32[32,8]{1,0:T(8,128)} async-done(((f32[1024,8]{1,0:T(8,128)}), f32[32,8]{1,0:T(8,128)}) %reduce-scatter.33.cloned.1.call-update) | async-done | bytes 1040
  1411.0 138.9 %reduce-scatter.23.cloned.1.call-done = f32[32,1024]{1,0:T(8,128)} async-done(((f32[1024,1024]{1,0:T(8,128)}), f32[32,1024]{1,0:T(8,128)}) %reduce-scatter.23.cloned.1.call-update) | async-done | bytes 131088 | tf_op jit(solution)/shard_map/reduce_scatter | solution.py:382
  1549.9 140.1 %reduce-scatter.21.cloned.1.call-done = f32[32,1024]{1,0:T(8,128)} async-done(((f32[1024,1024]{1,0:T(8,128)}), f32[32,1024]{1,0:T(8,128)}) %reduce-scatter.21.cloned.1.call-update) | async-done | bytes 131088 | tf_op jit(solution)/shard_map/reduce_scatter | solution.py:380
  1690.0 153.4 %reduce-scatter.25.cloned.1.call-done = f32[32,2816]{1,0:T(8,128)} async-done(((f32[1024,2816]{1,0:T(8,128)}), f32[32,2816]{1,0:T(8,128)}) %reduce-scatter.25.cloned.1.call-update) | async-done | bytes 360464 | tf_op jit(solution)/shard_map/reduce_scatter | solution.py:307
  1843.3 155.8 %reduce-scatter.27.cloned.1.call-done = f32[32,2816]{1,0:T(8,128)} async-done(((f32[1024,2816]{1,0:T(8,128)}), f32[32,2816]{1,0:T(8,128)}) %reduce-scatter.27.cloned.1.call-update) | async-done | bytes 360464 | tf_op jit(solution)/shard_map/reduce_scatter | solution.py:308
  1999.1 155.5 %reduce-scatter.29.cloned.1.call-done = f32[88,1024]{1,0:T(8,128)} async-done(((f32[2816,1024]{1,0:T(8,128)}), f32[88,1024]{1,0:T(8,128)}) %reduce-scatter.29.cloned.1.call-update) | async-done | bytes 360464 | tf_op jit(solution)/shard_map/reduce_scatter | solution.py:309
  2154.5 141.9 %reduce-scatter.17.cloned.1.call-done = f32[32,1024]{1,0:T(8,128)} async-done(((f32[1024,1024]{1,0:T(8,128)}), f32[32,1024]{1,0:T(8,128)}) %reduce-scatter.17.cloned.1.call-update) | async-done | bytes 131088 | tf_op jit(solution)/shard_map/reduce_scatter | solution.py:376
  2296.5 140.1 %reduce-scatter.15.cloned.1.call-done = f32[32,1024]{1,0:T(8,128)} async-done(((f32[1024,1024]{1,0:T(8,128)}), f32[32,1024]{1,0:T(8,128)}) %reduce-scatter.15.cloned.1.call-update) | async-done | bytes 131088 | tf_op jit(solution)/shard_map/reduce_scatter | solution.py:375
  2436.5 140.1 %reduce-scatter.19.cloned.1.call-done = f32[32,1024]{1,0:T(8,128)} async-done(((f32[1024,1024]{1,0:T(8,128)}), f32[32,1024]{1,0:T(8,128)}) %reduce-scatter.19.cloned.1.call-update) | async-done | bytes 131088 | tf_op jit(solution)/shard_map/reduce_scatter | solution.py:377
  (887 shorter events, 704.4 us)
Async XLA Ops:
  7.2 132.4 %copy-start.2 = (bf16[256,1024]{1,0:T(8,128)(2,1)S(1)}, bf16[256,1024]{1,0:T(8,128)(2,1)}, u32[]{:S(2)}) copy-start(bf16[256,1024]{1,0:T(8,128)(2,1)} %param.28) | copy-start | bytes 1572868
  7.2 129.8 %all-gather.23.cloned.1.call-start = ((), (), s32[]{:S(2)}) async-start(), calls=%async_computation.12 | async-start | bytes 2162688 | tf_op jit(solution)/shard_map/all_gather | solution.py:216
  7.9 131.6 %all-gather.21.cloned.1.call-start = ((), (), s32[]{:S(2)}) async-start(), calls=%async_computation.11 | async-start | bytes 2162688 | tf_op jit(solution)/shard_map/all_gather | solution.py:215
  8.7 177.9 %all-gather.19.cloned.1.call-start = ((), (), s32[]{:S(2)}) async-start(), calls=%async_computation.10 | async-start | bytes 2162688 | tf_op jit(solution)/shard_map/all_gather | solution.py:214
  9.4 365.3 %all-gather.35.cloned.1.call-start = ((), (), s32[]{:S(2)}) async-start(), calls=%async_computation.26 | async-start | bytes 17301504 | tf_op jit(solution)/shard_map/all_gather | solution.py:23
  134.0 58.4 %copy-start.91 = (f32[256]{0:T(256)}, f32[256]{0:T(256)S(1)}, u32[]{:S(2)}) copy-start(f32[256]{0:T(256)S(1)} %get-tuple-element.1429) | copy-start | bytes 3076
  135.4 57.1 %copy-start.93 = (f32[256]{0:T(256)}, f32[256]{0:T(256)S(1)}, u32[]{:S(2)}) copy-start(f32[256]{0:T(256)S(1)} %get-tuple-element.1457) | copy-start | bytes 3076
  135.4 57.1 %copy-start.95 = (f32[256]{0:T(256)}, f32[256]{0:T(256)S(1)}, u32[]{:S(2)}) copy-start(f32[256]{0:T(256)S(1)} %get-tuple-element.1458) | copy-start | bytes 3076
  136.9 55.6 %copy-start.77 = (f32[1,3072]{1,0:T(1,128)}, f32[1,3072]{1,0:T(1,128)S(1)}, u32[]{:S(2)}) copy-start(f32[1,3072]{1,0:T(1,128)S(1)} %get-tuple-element.1451) | copy-start | bytes 36868
  136.9 55.6 %copy-start.79 = (f32[1,3072]{1,0:T(1,128)}, f32[1,3072]{1,0:T(1,128)S(1)}, u32[]{:S(2)}) copy-start(f32[1,3072]{1,0:T(1,128)S(1)} %get-tuple-element.1452) | copy-start | bytes 36868
  136.9 55.6 %copy-start.81 = (f32[1,3072]{1,0:T(1,128)}, f32[1,3072]{1,0:T(1,128)S(1)}, u32[]{:S(2)}) copy-start(f32[1,3072]{1,0:T(1,128)S(1)} %get-tuple-element.1453) | copy-start | bytes 36868
  189.0 3.0 collective-permute-start
  257.8 232.7 %all-gather.37.cloned.1.call-start = ((), (), s32[]{:S(2)}) async-start(), calls=%async_computation.27 | async-start | bytes 17301504 | tf_op jit(solution)/shard_map/all_gather | solution.py:23
  258.9 518.1 %all-gather.25.cloned.1.call-start = ((), (), s32[]{:S(2)}) async-start(), calls=%async_computation.13 | async-start | bytes 2162688 | tf_op jit(solution)/shard_map/all_gather | solution.py:219
  259.4 522.8 %all-gather.27.cloned.1.call-start = ((), (), s32[]{:S(2)}) async-start(), calls=%async_computation.14 | async-start | bytes 2162688 | tf_op jit(solution)/shard_map/all_gather | solution.py:221
  260.2 525.8 %all-gather.29.cloned.1.call-start = ((), (), s32[]{:S(2)}) async-start(), calls=%async_computation.15 | async-start | bytes 5947392 | tf_op jit(solution)/shard_map/all_gather | solution.py:273
  260.9 531.1 %all-gather.31.cloned.1.call-start = ((), (), s32[]{:S(2)}) async-start(), calls=%async_computation.16 | async-start | bytes 5947392 | tf_op jit(solution)/shard_map/all_gather | solution.py:274
  261.7 551.5 %all-gather.33.cloned.1.call-start = ((), (), s32[]{:S(2)}) async-start(), calls=%async_computation.17 | async-start | bytes 5947392 | tf_op jit(solution)/shard_map/all_gather | solution.py:275
  262.3 638.8 %all-gather.39.cloned.1.call-start = ((), (), s32[]{:S(2)}) async-start(), calls=%async_computation.28 | async-start | bytes 8650752 | tf_op jit(solution)/shard_map/all_gather | solution.py:43
  262.6 227.9 %copy-start.70 = (f32[256,8]{1,0:T(8,128)}, f32[256,8]{1,0:T(8,128)S(1)}, u32[]{:S(2)}) copy-start(f32[256,8]{1,0:T(8,128)S(1)} %copy.453) | copy-start | bytes 24580
  265.2 711.9 %all-gather.41.cloned.1.call-start = ((), (), s32[]{:S(2)}) async-start(), calls=%async_computation.29 | async-start | bytes 8650752 | tf_op jit(solution)/shard_map/all_gather | solution.py:43
  900.3 384.5 %reduce-scatter.31.cloned.1.call-start = ((), (), s32[]{:S(2)}) async-start(), calls=%async_computation.30 | async-start | bytes 1622016
  1181.8 227.7 %reduce-scatter.33.cloned.1.call-start = ((), (), s32[]{:S(2)}) async-start(), calls=%async_computation.31 | async-start | bytes 540672
  1185.1 364.8 %reduce-scatter.23.cloned.1.call-start = ((), (), s32[]{:S(2)}) async-start(), calls=%async_computation.22 | async-start | bytes 4325376 | tf_op jit(solution)/shard_map/reduce_scatter | solution.py:382
  1187.9 502.1 %reduce-scatter.21.cloned.1.call-start = ((), (), s32[]{:S(2)}) async-start(), calls=%async_computation.21 | async-start | bytes 4325376 | tf_op jit(solution)/shard_map/reduce_scatter | solution.py:380
  1191.7 651.6 %reduce-scatter.25.cloned.1.call-start = ((), (), s32[]{:S(2)}) async-start(), calls=%async_computation.23 | async-start | bytes 11894784 | tf_op jit(solution)/shard_map/reduce_scatter | solution.py:307
  1199.2 799.9 %reduce-scatter.27.cloned.1.call-start = ((), (), s32[]{:S(2)}) async-start(), calls=%async_computation.24 | async-start | bytes 11894784 | tf_op jit(solution)/shard_map/reduce_scatter | solution.py:308
  1206.4 948.1 %reduce-scatter.29.cloned.1.call-start = ((), (), s32[]{:S(2)}) async-start(), calls=%async_computation.25 | async-start | bytes 11894784 | tf_op jit(solution)/shard_map/reduce_scatter | solution.py:309
  1213.9 1082.6 %reduce-scatter.17.cloned.1.call-start = ((), (), s32[]{:S(2)}) async-start(), calls=%async_computation.19 | async-start | bytes 4325376 | tf_op jit(solution)/shard_map/reduce_scatter | solution.py:376
  1219.8 3.1 collective-permute-start.1
  1225.7 1210.8 %reduce-scatter.15.cloned.1.call-start = ((), (), s32[]{:S(2)}) async-start(), calls=%async_computation.18 | async-start | bytes 4325376 | tf_op jit(solution)/shard_map/reduce_scatter | solution.py:375
  1228.8 1347.8 %reduce-scatter.19.cloned.1.call-start = ((), (), s32[]{:S(2)}) async-start(), calls=%async_computation.20 | async-start | bytes 4325376 | tf_op jit(solution)/shard_map/reduce_scatter | solution.py:377
  (109 other events, 623.1 us)
Sparse Core Ops, SparseCore 0:
  10.9 59.2 all-gather.22
  73.0 55.3 all-gather.20
  131.3 55.2 all-gather.18
  257.9 116.7 all-gather.34
  377.4 113.0 all-gather.36
  493.2 54.5 all-gather.24
  550.7 55.2 all-gather.26
  608.8 66.1 all-gather.28
  677.9 66.2 all-gather.30
  746.9 66.2 all-gather.32
  816.6 76.5 all-gather.38
  900.4 76.6 all-gather.40
  1182.0 92.8 reduce-scatter.30
  1277.0 132.5 reduce-scatter.32
  1412.4 137.4 reduce-scatter.22
  1552.7 137.2 reduce-scatter.20
  1692.8 150.4 reduce-scatter.24
  1846.2 152.8 reduce-scatter.26
  2002.1 152.4 reduce-scatter.28
  2157.3 139.0 reduce-scatter.16
  2299.4 137.0 reduce-scatter.14
  2439.5 137.0 reduce-scatter.18
where the time goes:
time: 2600 us; the launch traced here: 2580 us
  waiting for transfers between devices  1660 us (64%)
  matrix products  451 us (17%)
  local copies, waits for them, and re-layouts  248 us (10%)
  blocking collectives  157 us (6%)
  other arithmetic  43.3 us (2%)
    all_gather x2, waiting for transfers between devices, entering_2(): everything = jax.tree.map(lambda part: lax.all_gather(part, axis), array)  225 us
    reduce_scatter x1, waiting for transfers between devices, local(): lax.psum_scatter(mlp_terms[2], ('seq', 'fsdp'), scatter_dimension=0, tile...  156 us
    reduce_scatter x1, waiting for transfers between devices, local(): lax.psum_scatter(mlp_terms[3], ('seq', 'fsdp'), scatter_dimension=0, tile...  155 us
    reduce_scatter x1, waiting for transfers between devices, local(): lax.psum_scatter(mlp_terms[1], ('seq', 'fsdp'), scatter_dimension=0, tile...  153 us
    reduce_scatter x1, waiting for transfers between devices, local(): lax.psum_scatter(attn_terms[2], ('seq', 'fsdp'), scatter_dimension=0, til...  142 us
    reduce_scatter x1, waiting for transfers between devices, local(): lax.psum_scatter(attn_terms[3], ('seq', 'fsdp'), scatter_dimension=0, til...  140 us
    reduce_scatter x1, waiting for transfers between devices, local(): lax.psum_scatter(attn_terms[6], ('seq', 'fsdp'), scatter_dimension=0, til...  140 us
    reduce_scatter x1, waiting for transfers between devices, local(): lax.psum_scatter(attn_terms[1], ('seq', 'fsdp'), scatter_dimension=0, til...  140 us
  transfers between devices with their start and end apart: 24, of which 15 were waited for; matrix products, arithmetic and copies ran while one was open for 18% of the time, Pallas kernels for 0%

commit v1 on v0

v1 whole, which is shorter than its diff:
```python
from functools import partial

import jax
import jax.numpy as jnp
from jax import lax
from jax.experimental import pallas as pl
from jax.experimental.pallas import tpu as pltpu
from jax.sharding import PartitionSpec as P

CONV = 4
RIM = 8
LANES = 128
BASE = 16
SEQ, FSDP = "seq", "fsdp"
BOTH = (SEQ, FSDP)
f32 = jnp.float32
bf16 = jnp.bfloat16
highest = lax.Precision.HIGHEST
NN = (((1,), (0,)), ((), ()))
NT = (((1,), (1,)), ((), ()))
TN = (((0,), (0,)), ((), ()))


def mm(a, b, dims=NN, passes=6):
    if passes == 6:
        return lax.dot_general(a, b, dims, precision=highest, preferred_element_type=f32)
    a_high = a.astype(bf16)
    b_high = b.astype(bf16)
    out = lax.dot_general(a_high, b_high, dims, preferred_element_type=f32)
    if passes == 3:
        a_low = (a - a_high.astype(f32)).astype(bf16)
        b_low = (b - b_high.astype(f32)).astype(bf16)
        out = out + lax.dot_general(a_low, b_high, dims, preferred_element_type=f32)
        out = out + lax.dot_general(a_high, b_low, dims, preferred_element_type=f32)
    return out


def sigmoid(v):
    return 1.0 / (1.0 + jnp.exp(-v))


def iotas(rows):
    return (
        lax.broadcasted_iota(jnp.int32, (rows, rows), 0),
        lax.broadcasted_iota(jnp.int32, (rows, rows), 1),
    )


def unit_lower_inverse(lower, rows, cols, passes):
    size = lower.shape[0]
    same = (rows // BASE) == (cols // BASE)
    power = jnp.where(same, -lower, 0.0)
    inverse = jnp.where(rows == cols, 1.0, power)
    covered = 2
    while covered < BASE:
        power = mm(power, power, passes=passes)
        inverse = inverse + mm(inverse, power, passes=passes)
        covered *= 2
    block = BASE
    while block < size:
        joined = ((rows // (2 * block)) == (cols // (2 * block))) & (
            (rows // block) != (cols // block)
        )
        off = jnp.where(joined, lower, 0.0)
        inverse = inverse - mm(mm(inverse, off, passes=passes), inverse, passes=passes)
        block *= 2
    return inverse


def head_column(table, head):
    lanes = lax.broadcasted_iota(jnp.int32, table.shape, 1)
    return jnp.sum(jnp.where(lanes == head, table, 0.0), axis=1, keepdims=True)


def load_extended(ref, scratch, rows):
    scratch[0:RIM, :] = ref[rows : rows + RIM, :].astype(f32)
    scratch[RIM : RIM + rows, :] = ref[0:rows, :].astype(f32)


def convolve(scratch, taps, rows):
    total = taps[CONV - 1 : CONV, :] * scratch[RIM : RIM + rows, :]
    for j in range(CONV - 1):
        first = RIM - (CONV - 1) + j
        total = total + taps[j : j + 1, :] * scratch[first : first + rows, :]
    return total


FRONT_PASSES = 6
PASS_PASSES = 6
BACK_PASSES = 6


def front_kernel(
    pq, pk, pv, tq, tk, tv, beta_logit, q_out, k_out, v_out, t_out, l_out, b_out, scratch
):
    head = pl.program_id(0)
    rows = q_out.shape[0]
    active = []
    for ref, taps in ((pq, tq), (pk, tk), (pv, tv)):
        load_extended(ref, scratch, rows)
        c = convolve(scratch, taps, rows)
        active.append(c * sigmoid(c))
    a, b, v = active
    q_out[...] = a * lax.rsqrt(jnp.sum(a * a, axis=1, keepdims=True) + 1e-06)
    k = b * lax.rsqrt(jnp.sum(b * b, axis=1, keepdims=True) + 1e-06)
    k_out[...] = k
    v_out[...] = v
    beta = sigmoid(head_column(beta_logit[...], head))
    ri, ci = iotas(rows)
    lower = jnp.where(ri > ci, beta * mm(k, k, NT, FRONT_PASSES), 0.0)
    t = unit_lower_inverse(lower, ri, ci, FRONT_PASSES)
    t_out[0] = t
    u = mm(t, beta * v, NN, FRONT_PASSES)
    w = mm(t, beta * k, NN, FRONT_PASSES)
    size = k.shape[1]
    rs, cs = iotas(size)
    l_out[0] = jnp.where(rs == cs, 1.0, 0.0) - mm(w, k, TN, FRONT_PASSES)
    b_out[0] = mm(u, k, TN, FRONT_PASSES)


def pass_kernel(
    q_ref, k_ref, v_ref, t_ref, beta_logit, s_ref, gate_ref, gain_ref, branch_out, o_out, d_out, p_out
):
    head = pl.program_id(0)
    rows = q_ref.shape[0]
    q, k, s = q_ref[...], k_ref[...], s_ref[0]
    beta = sigmoid(head_column(beta_logit[...], head))
    ri, ci = iotas(rows)
    p = jnp.where(ri >= ci, mm(q, k, NT, PASS_PASSES), 0.0)
    p_out[0] = p
    missing = v_ref[...] - mm(k, s, NT, PASS_PASSES)
    d = mm(t_ref[0], beta * missing, NN, PASS_PASSES)
    d_out[...] = d
    o = mm(q, s, NT, PASS_PASSES) + mm(p, d, NN, PASS_PASSES)
    o_out[...] = o
    n = o * lax.rsqrt(jnp.mean(o * o, axis=1, keepdims=True) + 1e-05)
    g = gate_ref[...]
    branch_out[...] = (n * gain_ref[...] * (g * sigmoid(g))).astype(bf16)


def back_one_kernel(
    db_ref, o_ref, gate_ref, gain_ref, p_ref, t_ref, q_ref, k_ref, beta_logit,
    dgate_out, donorm_out, do_out, dr_out, g_out,
):
    head = pl.program_id(0)
    o = o_ref[...]
    g = gate_ref[...]
    gain = gain_ref[...]
    db = db_ref[...]
    beta = sigmoid(head_column(beta_logit[...], head))
    scale = lax.rsqrt(jnp.mean(o * o, axis=1, keepdims=True) + 1e-05)
    n = o * scale
    sig = sigmoid(g)
    z = g * sig
    dgate_out[...] = (db * n * gain * (sig * (1.0 + g * (1.0 - sig)))).astype(bf16)
    dy = db * z
    donorm_out[0] = jnp.sum(dy * n, axis=0, keepdims=True)
    dyg = dy * gain
    do = scale * dyg - o * (scale * scale * scale) * jnp.mean(dyg * o, axis=1, keepdims=True)
    do_out[...] = do
    dd = mm(p_ref[0], do, TN, BACK_PASSES)
    dr = mm(t_ref[0], dd, TN, BACK_PASSES)
    dr_out[...] = dr
    g_out[0] = mm(do, q_ref[...], TN, BACK_PASSES) - mm(beta * dr, k_ref[...], TN, BACK_PASSES)


def back_two_kernel(
    ds_ref, s_ref, t_ref, p_ref, q_ref, k_ref, v_ref, beta_logit, do_ref, dr_ref, d_ref,
    pq, pk, pv, tq, tk, tv,
    dq_out, dk_out, dv_out, rq_out, rk_out, rv_out, cq_out, ck_out, cv_out, dbeta_out,
    scratch, spread,
):
    head = pl.program_id(0)
    rows = q_ref.shape[0]
    ds, s = ds_ref[0], s_ref[0]
    q, k, v = q_ref[...], k_ref[...], v_ref[...]
    do, d = do_ref[...], d_ref[...]
    beta = sigmoid(head_column(beta_logit[...], head))
    ri, ci = iotas(rows)
    dr = dr_ref[...] + mm(t_ref[0], mm(k, ds, NT, BACK_PASSES), TN, BACK_PASSES)
    missing = v - mm(k, s, NT, BACK_PASSES)
    dp = jnp.where(ri >= ci, mm(do, d, NT, BACK_PASSES), 0.0)
    bdr = beta * dr
    dq = mm(do, s, NN, BACK_PASSES) + mm(dp, k, NN, BACK_PASSES)
    dk = mm(dp, q, TN, BACK_PASSES) + mm(d, ds, NN, BACK_PASSES) - mm(bdr, s, NN, BACK_PASSES)
    da = jnp.where(ri > ci, -mm(dr, d, NT, BACK_PASSES), 0.0)
    dbeta = jnp.sum(dr * missing, axis=1, keepdims=True) + jnp.sum(
        da * mm(k, k, NT, BACK_PASSES), axis=1, keepdims=True
    )
    dm = beta * da
    dk = dk + mm(dm, k, NN, BACK_PASSES) + mm(dm, k, TN, BACK_PASSES)
    dlogit = dbeta * beta * (1.0 - beta)

    @pl.when(head == 0)
    def _():
        dbeta_out[...] = jnp.zeros_like(dbeta_out)

    lanes = lax.broadcasted_iota(jnp.int32, dbeta_out.shape, 1)
    dbeta_out[...] = jnp.where(lanes == head, dlogit, dbeta_out[...])
    width = q.shape[1]
    spread[0:RIM, :] = jnp.zeros((RIM, width), f32)
    spread[RIM + rows : RIM + rows + RIM, :] = jnp.zeros((RIM, width), f32)
    sets = (
        (pq, tq, dq, q, dq_out, rq_out, cq_out),
        (pk, tk, dk, k, dk_out, rk_out, ck_out),
        (pv, tv, bdr, None, dv_out, rv_out, cv_out),
    )
    for proj, taps, du, unit, out, rim_out, tap_out in sets:
        load_extended(proj, scratch, rows)
        c = convolve(scratch, taps, rows)
        sig = sigmoid(c)
        if unit is not None:
            act = c * sig
            inv = lax.rsqrt(jnp.sum(act * act, axis=1, keepdims=True) + 1e-06)
            du = (du - unit * jnp.sum(unit * du, axis=1, keepdims=True)) * inv
        dc = du * (sig * (1.0 + c * (1.0 - sig)))
        spread[RIM : RIM + rows, :] = dc
        total = jnp.zeros((rows, width), f32)
        rim = jnp.zeros((RIM, width), f32)
        for j in range(CONV):
            lag = CONV - 1 - j
            tap = taps[j : j + 1, :]
            total = total + tap * spread[RIM + lag : RIM + lag + rows, :]
            rim = rim + tap * spread[lag : lag + RIM, :]
            first = RIM - lag
            tap_out[j : j + 1, :] = jnp.sum(
                dc * scratch[first : first + rows, :], axis=0, keepdims=True
            )
        out[...] = total
        rim_out[...] = rim


def params():
    return pltpu.CompilerParams(
        dimension_semantics=("arbitrary",), vmem_limit_bytes=48 * 1024 * 1024
    )


def column_block(rows, heads, part):
    return pl.BlockSpec((rows, LANES), lambda h, part=part: (0, part * heads + h))


def whole(shape):
    return pl.BlockSpec(shape, lambda h: (0,) * len(shape))


def per_head(shape):
    return pl.BlockSpec((1,) + shape, lambda h: (h, 0, 0))


def run_front(proj, taps, beta_logit, rows, heads):
    width = LANES
    p_spec = [column_block(rows + RIM, heads, i) for i in range(3)]
    t_spec = [column_block(CONV, heads, i) for i in range(3)]
    row_spec = column_block(rows, heads, 0)
    return pl.pallas_call(
        front_kernel,
        grid=(heads,),
        in_specs=p_spec + t_spec + [whole((rows, LANES))],
        out_specs=[row_spec] * 3
        + [per_head((rows, rows)), per_head((width, width)), per_head((width, width))],
        out_shape=[jax.ShapeDtypeStruct((rows, heads * width), f32)] * 3
        + [
            jax.ShapeDtypeStruct((heads, rows, rows), f32),
            jax.ShapeDtypeStruct((heads, width, width), f32),
            jax.ShapeDtypeStruct((heads, width, width), f32),
        ],
        scratch_shapes=[pltpu.VMEM((rows + RIM, width), f32)],
        compiler_params=params(),
        name="front",
    )(proj, proj, proj, taps, taps, taps, beta_logit)


def run_pass(q, k, v, t, beta_logit, states, gate, gain, rows, heads):
    width = LANES
    row_spec = column_block(rows, heads, 0)
    square = per_head((rows, rows))
    return pl.pallas_call(
        pass_kernel,
        grid=(heads,),
        in_specs=[
            row_spec, row_spec, row_spec, square, whole((rows, LANES)),
            per_head((width, width)), row_spec, whole((1, width)),
        ],
        out_specs=[row_spec, row_spec, row_spec, square],
        out_shape=[
            jax.ShapeDtypeStruct((rows, heads * width), bf16),
            jax.ShapeDtypeStruct((rows, heads * width), f32),
            jax.ShapeDtypeStruct((rows, heads * width), f32),
            jax.ShapeDtypeStruct((heads, rows, rows), f32),
        ],
        compiler_params=params(),
        name="chunk_pass",
    )(q, k, v, t, beta_logit, states, gate, gain)


def run_back_one(d_branch, o, gate, gain, p, t, q, k, beta_logit, rows, heads):
    width = LANES
    row_spec = column_block(rows, heads, 0)
    square = per_head((rows, rows))
    return pl.pallas_call(
        back_one_kernel,
        grid=(heads,),
        in_specs=[
            row_spec, row_spec, row_spec, whole((1, width)), square, square, row_spec, row_spec,
            whole((rows, LANES)),
        ],
        out_specs=[row_spec, per_head((1, width)), row_spec, row_spec, per_head((width, width))],
        out_shape=[
            jax.ShapeDtypeStruct((rows, heads * width), bf16),
            jax.ShapeDtypeStruct((heads, 1, width), f32),
            jax.ShapeDtypeStruct((rows, heads * width), f32),
            jax.ShapeDtypeStruct((rows, heads * width), f32),
            jax.ShapeDtypeStruct((heads, width, width), f32),
        ],
        compiler_params=params(),
        name="back_one",
    )(d_branch, o, gate, gain, p, t, q, k, beta_logit)


def run_back_two(ds, s, t, p, q, k, v, beta_logit, do, dr, d, proj, taps, rows, heads):
    width = LANES
    row_spec = column_block(rows, heads, 0)
    square = per_head((rows, rows))
    state = per_head((width, width))
    p_spec = [column_block(rows + RIM, heads, i) for i in range(3)]
    t_spec = [column_block(CONV, heads, i) for i in range(3)]
    return pl.pallas_call(
        back_two_kernel,
        grid=(heads,),
        in_specs=[
            state, state, square, square, row_spec, row_spec, row_spec, whole((rows, LANES)),
            row_spec, row_spec, row_spec,
        ]
        + p_spec
        + t_spec,
        out_specs=[row_spec] * 3
        + [column_block(RIM, heads, 0)] * 3
        + [column_block(CONV, heads, 0)] * 3
        + [whole((rows, LANES))],
        out_shape=[jax.ShapeDtypeStruct((rows, heads * width), f32)] * 3
        + [jax.ShapeDtypeStruct((RIM, heads * width), f32)] * 3
        + [jax.ShapeDtypeStruct((CONV, heads * width), f32)] * 3
        + [jax.ShapeDtypeStruct((rows, LANES), f32)],
        scratch_shapes=[
            pltpu.VMEM((rows + RIM, width), f32),
            pltpu.VMEM((rows + 2 * RIM, width), f32),
        ],
        compiler_params=params(),
        name="back_two",
    )(ds, s, t, p, q, k, v, beta_logit, do, dr, d, proj, proj, proj, taps, taps, taps)


def swap_parts(parts, axis):
    count = lax.axis_size(axis)
    place = lax.axis_index(axis)
    own = lax.dynamic_slice_in_dim(parts, place, 1, 0)
    result = jnp.zeros_like(parts)
    result = lax.dynamic_update_slice_in_dim(result, own, place, 0)
    for hop in range(1, count):
        target = lax.rem(place + hop, count)
        sent = lax.dynamic_slice_in_dim(parts, target, 1, 0)
        pairs = [(i, (i + hop) % count) for i in range(count)]
        got = lax.ppermute(sent, axis, pairs)
        source = lax.rem(place + count - hop, count)
        result = lax.dynamic_update_slice_in_dim(result, got, source, 0)
    return result


def bmm(a, b):
    return jnp.einsum("...ij,...jk->...ik", a, b, precision=highest)


def bmm_t(a, b):
    return jnp.einsum("...ij,...kj->...ik", a, b, precision=highest)


def shift_groups(array, by):
    size = lax.axis_size(SEQ)
    return lax.ppermute(
        array, SEQ, [(i, i + by) for i in range(size) if 0 <= i + by < size]
    )


def states_entering(linear, constant, before, reach):
    count = lax.axis_size(FSDP)
    heads, width = linear.shape[0], linear.shape[1]
    mine = heads // count
    pair = jnp.concatenate([linear, constant], axis=1).reshape(count, mine, 2 * width, width)
    pair = swap_parts(pair, FSDP)
    linears = [pair[i, :, :width] for i in range(count)]
    prefix = [pair[0]]
    for i in range(1, count):
        joined = bmm(prefix[-1], linears[i])
        prefix.append(
            jnp.concatenate(
                [joined[:, :width], joined[:, width:] + pair[i, :, width:]], axis=1
            )
        )
    group = prefix[-1]
    earlier = [shift_groups(group, hop) for hop in range(1, reach + 1)]
    state = jnp.zeros((mine, width, width), f32)
    for hop in range(reach, 0, -1):
        total = earlier[hop - 1]
        state = bmm(state, total[:, :width]) + total[:, width:]
        state = jnp.where(hop <= before, state, 0.0)
    entries = [state]
    for i in range(1, count):
        entries.append(bmm(state, prefix[i - 1][:, :width]) + prefix[i - 1][:, width:])
    entering = swap_parts(jnp.stack(entries), FSDP).reshape(heads, width, width)
    later = [shift_groups(group[:, :width], -hop) for hop in range(1, reach + 1)]
    return entering, linears, later


def state_grads_leaving(grads, linears, later, after, reach):
    count = lax.axis_size(FSDP)
    heads, width = grads.shape[0], grads.shape[1]
    mine = heads // count
    parts = swap_parts(grads.reshape(count, mine, width, width), FSDP)
    inner = [None] * count
    inner[count - 1] = jnp.zeros((mine, width, width), f32)
    tails = [None] * count
    for i in range(count - 2, -1, -1):
        inner[i] = bmm_t(inner[i + 1], linears[i + 1]) + parts[i + 1]
        tails[i] = (
            linears[i + 1] if tails[i + 1] is None else bmm(linears[i + 1], tails[i + 1])
        )
    group = bmm_t(inner[0], linears[0]) + parts[0]
    beyond = [shift_groups(group, -hop) for hop in range(1, reach + 1)]
    state = jnp.zeros((mine, width, width), f32)
    for hop in range(reach, 0, -1):
        state = bmm_t(state, later[hop - 1]) + beyond[hop - 1]
        state = jnp.where(hop <= after, state, 0.0)
    entries = [inner[i] + bmm_t(state, tails[i]) for i in range(count - 1)] + [state]
    return swap_parts(jnp.stack(entries), FSDP).reshape(heads, width, width)


def rms(values):
    return lax.rsqrt(jnp.mean(values * values, axis=-1, keepdims=True) + 1e-05)


def rms_back(values, scale, gain, dy):
    dyg = dy * gain
    grad = scale * dyg - values * (scale * scale * scale) * jnp.mean(
        dyg * values, axis=-1, keepdims=True
    )
    return grad, jnp.sum(dy * values * scale, axis=0)


def dot(a, b):
    return jnp.dot(a, b, preferred_element_type=f32)


def dot_t(a, b):
    return lax.dot_general(a, b, NT, preferred_element_type=f32)


def t_dot(a, b):
    return lax.dot_general(a, b, TN, preferred_element_type=f32)


def local(
    tokens, attn_gain, w_query, w_key, w_value, conv_weight, w_beta, w_gate_out, onorm_gain,
    w_out, mlp_gain, w_mlp_gate, w_mlp_up, w_down, seq_lengths, cotangent,
):
    rows, model = tokens.shape
    heads = w_beta.shape[1]
    hidden_size = w_mlp_gate.shape[1]
    devices = lax.axis_size(BOTH)
    share = model // devices
    groups = lax.axis_size(SEQ)
    reach = groups // 2 - 1
    width = model // heads
    chan = 3 * model
    taps_per_row = CONV * 3

    group_rows = rows * lax.axis_size(FSDP)
    first = lax.axis_index(BOTH) * rows
    group_first = lax.axis_index(SEQ) * group_rows
    ends = jnp.cumsum(seq_lengths)
    starts = ends - seq_lengths
    begin = jnp.max(jnp.where(starts <= first, starts, 0))
    end = jnp.min(jnp.where(ends > first, ends, rows * devices))
    opens = first == begin
    before = (group_first - begin) // group_rows
    after = (end - group_first) // group_rows - 1

    misc = jnp.zeros((share, LANES), bf16)
    misc = misc.at[:, :heads].set(w_beta)
    misc = misc.at[:, heads].set(attn_gain)
    misc = misc.at[:, heads + 1].set(mlp_gain)
    misc = misc.at[:, heads + 2 : heads + 2 + taps_per_row].set(
        conv_weight.reshape(share, taps_per_row)
    )
    misc = misc.at[: onorm_gain.shape[0], heads + 2 + taps_per_row].set(onorm_gain)
    pack_one = jnp.concatenate([w_query, w_key, w_value, misc], axis=1)
    full_one = lax.all_gather(pack_one, BOTH, axis=0, tiled=True)
    pack_two = jnp.concatenate([w_gate_out, w_out, w_mlp_gate, w_mlp_up], axis=1)
    pack_two, full_one = lax.optimization_barrier((pack_two, full_one))
    full_two = lax.all_gather(pack_two, BOTH, axis=0, tiled=True)
    w_down, full_two = lax.optimization_barrier((w_down, full_two))
    full_down = lax.all_gather(w_down, BOTH, axis=0, tiled=True)

    w_qkv = full_one[:, :chan]
    full_misc = full_one[:, chan:]
    gain_one = full_misc[:, heads].astype(f32)
    gain_two = full_misc[:, heads + 1].astype(f32)
    taps = (
        full_misc[:, heads + 2 : heads + 2 + taps_per_row]
        .reshape(devices, CONV, chan // devices)
        .swapaxes(0, 1)
        .reshape(CONV, chan)
        .astype(f32)
    )
    onorm = (
        full_misc[:, heads + 2 + taps_per_row]
        .reshape(devices, share)[:, : onorm_gain.shape[0]]
        .reshape(1, width)
        .astype(f32)
    )
    w_gate_full = full_two[:, :model]
    w_out_full = full_two[:, model : 2 * model]
    w_mg = full_two[:, 2 * model : 2 * model + hidden_size]
    w_mu = full_two[:, 2 * model + hidden_size :]

    rim_tokens = lax.ppermute(
        tokens[rows - RIM :], BOTH, [(i, i + 1) for i in range(devices - 1)]
    )
    rim_tokens = jnp.where(opens, jnp.zeros_like(rim_tokens), rim_tokens)
    x_all = jnp.concatenate([tokens, rim_tokens], axis=0).astype(f32)
    scale_all = rms(x_all)
    normed_all = (x_all * scale_all * gain_one).astype(bf16)
    projected = dot(normed_all, w_qkv).astype(bf16)
    normed = normed_all[:rows]
    x = tokens.astype(f32)
    scale_one = scale_all[:rows]
    beta_logit = dot(normed, full_misc)
    q, k, v, t, linear, constant = run_front(projected, taps, beta_logit, rows, heads)
    entering, linears, later = states_entering(linear, constant, before, reach)
    gate_logit = dot(normed, w_gate_full)
    branch, o, d, p = run_pass(
        q, k, v, t, beta_logit, entering, gate_logit, onorm, rows, heads
    )
    hidden = x + dot(branch, w_out_full)
    scale_two = rms(hidden)
    normed_two = (hidden * scale_two * gain_two).astype(bf16)
    gate_rows = dot(normed_two, w_mg)
    up_rows = dot(normed_two, w_mu)
    sig = sigmoid(gate_rows)
    act = gate_rows * sig
    inner = (act * up_rows).astype(bf16)
    output = (hidden + dot(inner, full_down)).astype(bf16)

    d_inner = dot_t(cotangent, full_down)
    d_gate = (d_inner * up_rows * (sig * (1.0 + gate_rows * (1.0 - sig)))).astype(bf16)
    d_up = (d_inner * act).astype(bf16)
    grad_down = t_dot(inner, cotangent).astype(bf16)
    grad_mg = t_dot(normed_two, d_gate).astype(bf16)
    grad_mu = t_dot(normed_two, d_up).astype(bf16)
    d_normed_two = dot_t(d_gate, w_mg) + dot_t(d_up, w_mu)
    d_norm, grad_gain_two = rms_back(hidden, scale_two, gain_two, d_normed_two)
    d_hidden = cotangent.astype(f32) + d_norm
    d_attn = d_hidden.astype(bf16)
    d_branch = dot_t(d_attn, w_out_full)
    grad_wout = t_dot(branch, d_attn).astype(bf16)

    d_gate_logit, d_onorm, d_o, d_r, state_grad = run_back_one(
        d_branch, o, gate_logit, onorm, p, t, q, k, beta_logit, rows, heads
    )
    leaving = state_grads_leaving(state_grad, linears, later, after, reach)
    grad_wgate = t_dot(normed, d_gate_logit).astype(bf16)
    outs = run_back_two(
        leaving, entering, t, p, q, k, v, beta_logit, d_o, d_r, d, projected, taps, rows, heads
    )
    d_local = outs[0:3]
    rims = jnp.concatenate(outs[3:6], axis=1)
    d_taps = jnp.concatenate(outs[6:9], axis=1)
    d_beta = outs[9].astype(bf16)
    rims = jnp.where(opens, jnp.zeros_like(rims), rims)
    rims = lax.ppermute(rims, BOTH, [(i + 1, i) for i in range(devices - 1)])
    d_cols = []
    for i in range(3):
        part = d_local[i]
        tail = part[rows - RIM :] + rims[:, i * model : (i + 1) * model]
        d_cols.append(jnp.concatenate([part[: rows - RIM], tail], axis=0).astype(bf16))
    d_proj = jnp.concatenate(d_cols, axis=1)
    grad_qkv = t_dot(normed, d_proj).astype(bf16)
    grad_beta = t_dot(normed, d_beta)[:, :heads]
    beta_cols = jnp.where(
        lax.broadcasted_iota(jnp.int32, full_misc.shape, 1) < heads, full_misc, 0
    )
    d_normed = dot_t(d_proj, w_qkv) + dot_t(d_beta, beta_cols) + dot_t(d_gate_logit, w_gate_full)
    d_token_norm, grad_gain_one = rms_back(x, scale_one, gain_one, d_normed)
    grad_tokens = d_hidden + d_token_norm

    grad_misc = jnp.zeros((model, LANES), f32)
    grad_misc = grad_misc.at[:, :heads].set(grad_beta)
    grad_misc = grad_misc.at[:, heads].set(grad_gain_one)
    grad_misc = grad_misc.at[:, heads + 1].set(grad_gain_two)
    grad_misc = grad_misc.at[:, heads + 2 : heads + 2 + taps_per_row].set(
        d_taps.reshape(CONV, devices, chan // devices).swapaxes(0, 1).reshape(model, taps_per_row)
    )
    own_gain = onorm_gain.shape[0]
    onorm_cols = jnp.zeros((devices, share), f32)
    onorm_cols = onorm_cols.at[:, :own_gain].set(
        jnp.sum(d_onorm, axis=(0, 1)).reshape(devices, own_gain)
    )
    grad_misc = grad_misc.at[:, heads + 2 + taps_per_row].set(onorm_cols.reshape(model))

    def scattered(term):
        return lax.psum_scatter(term, BOTH, scatter_dimension=0, tiled=True).astype(f32)

    g_mlp = scattered(jnp.concatenate([grad_mg, grad_mu], axis=1))
    g_down = scattered(grad_down)
    g_attn = scattered(
        jnp.concatenate([grad_qkv, grad_wgate, grad_wout, grad_misc.astype(bf16)], axis=1)
    )
    g_misc = g_attn[:, 5 * model :]
    return (
        output,
        grad_tokens,
        g_misc[:, heads],
        g_attn[:, :model],
        g_attn[:, model : 2 * model],
        g_attn[:, 2 * model : 3 * model],
        g_misc[:, heads + 2 : heads + 2 + taps_per_row].reshape(CONV, chan // devices),
        g_misc[:, :heads],
        g_attn[:, 3 * model : 4 * model],
        g_misc[:own_gain, heads + 2 + taps_per_row],
        g_attn[:, 4 * model : 5 * model],
        g_misc[:, heads + 1],
        g_mlp[:, :hidden_size],
        g_mlp[:, hidden_size:],
        g_down,
    )


def solution(mesh):
    rows = P(BOTH, None)
    flat = P(BOTH)
    cols = P(None, BOTH)
    return jax.shard_map(
        local,
        mesh=mesh,
        in_specs=(
            rows, flat, rows, rows, rows, cols, rows, rows, flat, rows, flat, rows, rows, rows,
            P(), rows,
        ),
        out_specs=(
            rows, rows, flat, rows, rows, rows, cols, rows, rows, flat, rows, flat, rows, rows,
            rows,
        ),
        check_vma=False,
    )
```

time: 2600 us -> 868 us (0.33)
  waiting for transfers between devices: 1660 us -> 516 us
  matrix products: 451 us -> 92.2 us
  local copies, waits for them, and re-layouts: 248 us -> 31.8 us
  blocking collectives: 157 us -> 0 us
  Pallas kernels: 0 us -> 123 us
  starting transfers between devices: 4.71 us -> 33.3 us
    reduce_scatter x8 -> x3, waiting for transfers between devices: 1170 us -> 287 us  [scattered(): lax.psum_scatter(term, BOTH, scatter_dimension=0, tiled=True).astype(f32)]
    dot_general x238 -> x42, matrix products: 450 us -> 92.2 us  [the longest x7 31.3 us: dot(): return jnp.dot(a, b, preferred_element_type=f32)]
    all_gather x12 -> x3, waiting for transfers between devices: 361 us -> 184 us  [the longest x1 112 us: local(): full_two = lax.all_gather(pack_two, BOTH, axis=0, tiled=True)]
    dynamic_slice x138 -> x4, local copies, waits for them, and re-layouts: 143 us -> 0.91 us  [swap_parts(): sent = lax.dynamic_slice_in_dim(parts, target, 1, 0)]
    unnamed x24 -> x6, waiting for transfers between devices: 129 us -> 0.1 us
    pallas_call x0 -> x4, Pallas kernels: none -> 123 us  [the longest x1 63.7 us: run_front(): pl.pallas_call(front_kernel, grid=(heads,), in_specs=p_spec + t_spec + [w...]
    unnamed x2 -> x0, blocking collectives: 79.3 us -> none
    all_gather x2 -> x0, blocking collectives: 77.9 us -> none  [the longest x1 40.5 us: local(): lax.all_gather(conv_weight, ('seq', 'fsdp'), axis=1, tiled=True)]
  transfers between devices with their start and end apart: 24 -> 29, of which waited for: 15 -> 18; matrix products, arithmetic and copies ran while one was open for 18% -> 17% of each run, Pallas kernels for 0% -> 14%
where the time goes in v1:
time: 868 us; the launch traced here: 859 us
  waiting for transfers between devices  516 us (59%)
  Pallas kernels  123 us (14%)
  matrix products  92.2 us (11%)
  other arithmetic  45 us (5%)
  starting transfers between devices  33.3 us (4%)
  local copies, waits for them, and re-layouts  31.8 us (4%)
  between operations  17.8 us (2%)
    reduce_scatter x3, waiting for transfers between devices, scattered(): lax.psum_scatter(term, BOTH, scatter_dimension=0, tiled=True).astype(f32)  287 us
    all_gather x1, waiting for transfers between devices, local(): full_two = lax.all_gather(pack_two, BOTH, axis=0, tiled=True)  112 us
    all_gather x1, waiting for transfers between devices, local(): full_one = lax.all_gather(pack_one, BOTH, axis=0, tiled=True)  71.5 us
    pallas_call x1, Pallas kernels, run_front(): pl.pallas_call(front_kernel, grid=(heads,), in_specs=p_spec + t_spec + [w...  63.7 us
    dot_general x7, matrix products, dot(): return jnp.dot(a, b, preferred_element_type=f32)  31.3 us
    pallas_call x1, Pallas kernels, run_back_two(): pl.pallas_call(back_two_kernel, grid=(heads,), in_specs=[state, state, sq...  30.1 us
    dot_general x7, matrix products, dot_t(): return lax.dot_general(a, b, NT, preferred_element_type=f32)  26.6 us
    ppermute x9, waiting for transfers between devices, shift_groups(): lax.ppermute(array, SEQ, [(i, i + by) for i in range(size) if 0 <= i + by...  24.1 us
  transfers between devices with their start and end apart: 29, of which 18 were waited for; matrix products, arithmetic and copies ran while one was open for 17% of the time, Pallas kernels for 14%

profile of v1, /device:TPU:0, one launch (start us, length us, event | category | flops | bytes accessed | tf_op | source)
XLA Modules:
  0.0 858.8 jit_solution(7184652154294257118)
XLA Ops:
  25.2 71.5 %all-gather.4.cloned.1.call-done = bf16[1024,3200]{1,0:T(8,128)(2,1)} async-done(((bf16[32,3200]{1,0:T(8,128)(2,1)}), bf16[1024,3200]{1,0:T(8,128)(2,1)}) %all-gather.4.cloned.1.call-update) | async-done | bytes 6553616 | tf_op jit(solution)/shard_map/all_gather | solution.py:497
  96.7 112.0 %all-gather.6.cloned.1.call-done = bf16[1024,7680]{1,0:T(8,128)(2,1)} async-done(((bf16[32,7680]{1,0:T(8,128)(2,1)}), bf16[1024,7680]{1,0:T(8,128)(2,1)}) %all-gather.6.cloned.1.call-update) | async-done | bytes 15728656 | tf_op jit(solution)/shard_map/all_gather | solution.py:500
  220.4 4.6 fusion.12.pq.pk.pv
  225.1 63.7 %front.1 = (f32[256,1024]{1,0:T(8,128)S(1)}, f32[256,1024]{1,0:T(8,128)S(1)}, f32[256,1024]{1,0:T(8,128)S(1)}, f32[8,256,256]{2,1,0:T(8,128)}, f32[8,128,128]{2,1,0:T(8,128)S(1)}, /*index=5*/f32[8,128,128]{2,1,0:T(8,128)S(1)}) custom-call(bf16[264,3072]{1,0:T(8,128)(2,1)S(1)} %fusion.12.pq.pk.pv, bf16[264,3072]{1,0:T(8,128)(2,1)S(1)} %fusion.12.pq.pk.pv, ...), custom_call_target="tpu_custom_call" | custom-call | tf_op jit(solution)/shard_map/front/pallas_call | solution.py:256
  306.4 3.2 collective-permute-start.4
  310.8 3.5 collective-permute-start.5
  334.9 3.5 fusion.22.gate_ref
  338.4 14.8 %chunk_pass.1 = (bf16[256,1024]{1,0:T(8,128)(2,1)S(1)}, f32[256,1024]{1,0:T(8,128)S(1)}, f32[256,1024]{1,0:T(8,128)S(1)}, f32[8,256,256]{2,1,0:T(8,128)}) custom-call(f32[256,1024]{1,0:T(8,128)S(1)} %get-tuple-element.177.q_ref, f32[256,1024]{1,0:T(8,128)S(1)} %copy-done.4, f32[256,1024]{1,0:T(8,128)} %copy-done.5, f32[8,256,256]{2,1,0:T(8,128)} %get-tuple-element.180.t_ref, ...), custom_call_target="tpu_custom_call" | custom-call | tf_op jit(solution)/shard_map/chunk_pass/pallas_call | solution.py:278
  353.2 3.2 multiply_reduce_fusion.2
  356.6 6.3 fusion.6
  363.0 4.5 convolution_bitcast_fusion
  367.5 6.9 multiply_convert_fusion.1
  375.5 4.1 convolution_convert_fusion
  383.0 4.9 fusion.4
  387.8 4.5 multiply_reduce_fusion
  392.7 2.7 fusion.16.db_ref
  395.5 14.2 %back_one.1 = (bf16[256,1024]{1,0:T(8,128)(2,1)S(1)}, f32[8,1,128]{2,1,0:T(1,128)S(1)}, f32[256,1024]{1,0:T(8,128)S(1)}, f32[256,1024]{1,0:T(8,128)S(1)}, f32[8,128,128]{2,1,0:T(8,128)S(1)}) custom-call(f32[256,1024]{1,0:T(8,128)S(1)} %fusion.16.db_ref, f32[256,1024]{1,0:T(8,128)S(1)} %copy-done.10, f32[256,1024]{1,0:T(8,128)} %fusion.22.gate_ref, ...), custom_call_target="tpu_custom_call" | custom-call | tf_op jit(solution)/shard_map/back_one/pallas_call | solution.py:301
  414.8 4.8 collective-permute-done.11
  419.6 2.9 collective-permute-done.12
  430.8 13.7 %collective-permute-done.14 = f32[2,128,128]{2,1,0:T(8,128)S(1)} collective-permute-done((f32[2,128,128]{2,1,0:T(8,128)}, f32[2,128,128]{2,1,0:T(8,128)S(1)}, u32[]{:S(2)}, u32[]{:S(2)}) %collective-permute-start.14) | collective-permute-done | bytes 131104 | tf_op jit(solution)/shard_map/ppermute | solution.py:380
  445.8 6.9 collective-permute-done.16
  466.0 2.8 collective-permute-done.21
  468.9 30.1 %back_two.1 = (f32[256,1024]{1,0:T(8,128)S(1)}, f32[256,1024]{1,0:T(8,128)S(1)}, f32[256,1024]{1,0:T(8,128)S(1)}, f32[8,1024]{1,0:T(8,128)S(1)}, f32[8,1024]{1,0...) custom-call(f32[8,128,128]{2,1,0:T(8,128)S(1)} %bitcast.133, ...), custom_call_target="tpu_custom_call" | custom-call | tf_op jit(solution)/shard_map/back_two/pallas_call | solution.py:328
  506.6 5.2 fusion.29
  511.8 3.6 fusion.56
  523.5 3.2 convolution_convert_fusion.3
  526.8 5.5 pad_maximum_fusion.1
  533.3 3.1 convolution_convert_fusion.1
  538.1 7.0 pad_maximum_fusion
  546.9 5.3 fusion.35
  555.2 139.9 %reduce-scatter.4.cloned.1.call-done = bf16[32,5248]{1,0:T(8,128)(2,1)} async-done(((bf16[1024,5248]{1,0:T(8,128)(2,1)}), bf16[32,5248]{1,0:T(8,128)(2,1)}) %reduce-scatter.4.cloned.1.call-update) | async-done | bytes 335888 | tf_op jit(solution)/shard_map/reduce_scatter | solution.py:611
  702.2 147.4 %reduce-scatter.6.cloned.1.call-done = bf16[32,5632]{1,0:T(8,128)(2,1)} async-done(((bf16[1024,5632]{1,0:T(8,128)(2,1)}), bf16[32,5632]{1,0:T(8,128)(2,1)}) %reduce-scatter.6.cloned.1.call-update) | async-done | bytes 360464 | tf_op jit(solution)/shard_map/reduce_scatter | solution.py:611
  (278 shorter events, 131.5 us)
Async XLA Ops:
  7.2 211.6 %copy-start.22 = (bf16[256,1024]{1,0:T(8,128)(2,1)S(1)}, bf16[256,1024]{1,0:T(8,128)(2,1)}, u32[]{:S(2)}) copy-start(bf16[256,1024]{1,0:T(8,128)(2,1)} %param.38) | copy-start | bytes 1572868
  7.2 89.5 %all-gather.4.cloned.1.call-start = ((), (), s32[]{:S(2)}) async-start(), calls=%async_computation.3 | async-start | bytes 6758400 | tf_op jit(solution)/shard_map/all_gather | solution.py:497
  23.3 185.5 %all-gather.6.cloned.1.call-start = ((), (), s32[]{:S(2)}) async-start(), calls=%async_computation.4 | async-start | bytes 16220160 | tf_op jit(solution)/shard_map/all_gather | solution.py:500
  96.7 266.3 %all-gather.8.cloned.1.call-start = ((), (), s32[]{:S(2)}) async-start(), calls=%async_computation.5 | async-start | bytes 5947392 | tf_op jit(solution)/shard_map/all_gather | solution.py:502
  208.8 344.7 %reduce-scatter.8.cloned.1.call-start = ((), (), s32[]{:S(2)}) async-start(), calls=%async_computation.8 | async-start | bytes 5947392 | tf_op jit(solution)/shard_map/reduce_scatter | solution.py:611
  209.6 5.0 collective-permute-start
  225.1 63.8 %copy-start = (bf16[264,3072]{1,0:T(8,128)(2,1)}, bf16[264,3072]{1,0:T(8,128)(2,1)S(1)}, u32[]{:S(2)}) copy-start(bf16[264,3072]{1,0:T(8,128)(2,1)S(1)} %fusion.12.pq.pk.pv) | copy-start | bytes 4866052
  288.8 49.6 %copy-start.1 = (f32[256,1024]{1,0:T(8,128)}, f32[256,1024]{1,0:T(8,128)S(1)}, u32[]{:S(2)}) copy-start(f32[256,1024]{1,0:T(8,128)S(1)} %get-tuple-element.177.q_ref) | copy-start | bytes 3145732
  290.2 8.1 collective-permute-start.1
  291.6 9.3 %collective-permute-start.2 = (f32[1,2,256,128]{3,2,1,0:T(8,128)S(1)}, f32[1,2,256,128]{3,2,1,0:T(8,128)}, u32[]{:S(2)}, u32[]{:S(2)}) collective-permute-start(f32[1,2,256,128]{3,2,1,0:T(8,128)S(1)} %get-tuple-element.249), channel_id=1, source_target_pairs={{0,2},{1,3},{2,0},{3,1},{4,6},{5,7},{6,4},{7,5},{8,10},{9,11},{10,... | collective-permute-start | bytes 786440 | tf_op jit(solution)/shard_map/ppermute | solution.py:364
  293.0 10.5 %collective-permute-start.3 = (f32[1,2,256,128]{3,2,1,0:T(8,128)S(1)}, f32[1,2,256,128]{3,2,1,0:T(8,128)S(1)}, u32[]{:S(2)}, u32[]{:S(2)}) collective-permute-start(f32[1,2,256,128]{3,2,1,0:T(8,128)S(1)} %get-tuple-element.248), channel_id=1, source_target_pairs={{0,3},{1,0},{2,1},{3,2},{4,7},{5,4},{6,5},{7,6},{8,11},{9,8},{10,9... | collective-permute-start | bytes 786440 | tf_op jit(solution)/shard_map/ppermute | solution.py:364
  306.4 10.6 %collective-permute-start.4 = (f32[2,256,128]{2,1,0:T(8,128)S(1)}, f32[2,256,128]{2,1,0:T(8,128)}, u32[]{:S(2)}, u32[]{:S(2)}) collective-permute-start(f32[2,256,128]{2,1,0:T(8,128)S(1)} %pad_maximum_fusion.7), channel_id=1, source_target_pairs={{0,12},{4,16},{8,20},{12,24},{16,28},{1,13},{5,17},{9,21},{13,25},... | collective-permute-start | bytes 786440 | tf_op jit(solution)/shard_map/ppermute | solution.py:380
  310.8 8.6 %collective-permute-start.5 = (f32[2,256,128]{2,1,0:T(8,128)S(1)}, f32[2,256,128]{2,1,0:T(8,128)S(1)}, u32[]{:S(2)}, u32[]{:S(2)}) collective-permute-start(f32[2,256,128]{2,1,0:T(8,128)S(1)} %pad_maximum_fusion.7), channel_id=1, source_target_pairs={{0,8},{4,12},{8,16},{12,20},{16,24},{20,28},{1,9},{5,13},{9,17},{1... | collective-permute-start | bytes 786440 | tf_op jit(solution)/shard_map/ppermute | solution.py:380
  314.3 7.7 collective-permute-start.6
  324.0 6.9 collective-permute-start.7
  325.7 6.7 collective-permute-start.8
  327.0 102.5 %collective-permute-start.13 = (f32[2,128,128]{2,1,0:T(8,128)}, f32[2,128,128]{2,1,0:T(8,128)}, u32[]{:S(2)}, u32[]{:S(2)}) collective-permute-start(f32[2,128,128]{2,1,0:T(8,128)} %get-tuple-element.271), channel_id=1, source_target_pairs={{12,0},{16,4},{20,8},{24,12},{28,16},{13,1},{17,5},{21,9},{25,13},... | collective-permute-start | bytes 393224 | tf_op jit(solution)/shard_map/ppermute | solution.py:380
  328.3 117.5 %collective-permute-start.15 = (f32[2,128,128]{2,1,0:T(8,128)}, f32[2,128,128]{2,1,0:T(8,128)}, u32[]{:S(2)}, u32[]{:S(2)}) collective-permute-start(f32[2,128,128]{2,1,0:T(8,128)} %get-tuple-element.271), channel_id=1, source_target_pairs={{8,0},{12,4},{16,8},{20,12},{24,16},{28,20},{9,1},{13,5},{17,9},{2... | collective-permute-start | bytes 393224 | tf_op jit(solution)/shard_map/ppermute | solution.py:380
  329.6 124.4 %collective-permute-start.17 = (f32[2,128,128]{2,1,0:T(8,128)}, f32[2,128,128]{2,1,0:T(8,128)}, u32[]{:S(2)}, u32[]{:S(2)}) collective-permute-start(f32[2,128,128]{2,1,0:T(8,128)} %get-tuple-element.271), channel_id=1, source_target_pairs={{4,0},{8,4},{12,8},{16,12},{20,16},{24,20},{28,24},{5,1},{9,5},{13... | collective-permute-start | bytes 393224 | tf_op jit(solution)/shard_map/ppermute | solution.py:380
  330.9 4.0 collective-permute-start.9
  379.7 315.5 %reduce-scatter.4.cloned.1.call-start = ((), (), s32[]{:S(2)}) async-start(), calls=%async_computation.6 | async-start | bytes 11083776 | tf_op jit(solution)/shard_map/reduce_scatter | solution.py:611
  409.8 5.0 collective-permute-start.10
  410.3 9.2 %collective-permute-start.11 = (f32[1,2,128,128]{3,2,1,0:T(8,128)S(1)}, f32[1,2,128,128]{3,2,1,0:T(8,128)S(1)}, u32[]{:S(2)}, u32[]{:S(2)}) collective-permute-start(f32[1,2,128,128]{3,2,1,0:T(8,128)S(1)} %get-tuple-element.257), channel_id=1, source_target_pairs={{0,2},{1,3},{2,0},{3,1},{4,6},{5,7},{6,4},{7,5},{8,10},{9,11},{10,... | collective-permute-start | bytes 393224 | tf_op jit(solution)/shard_map/ppermute | solution.py:364
  414.8 7.6 collective-permute-start.12
  424.7 19.7 %collective-permute-start.14 = (f32[2,128,128]{2,1,0:T(8,128)}, f32[2,128,128]{2,1,0:T(8,128)S(1)}, u32[]{:S(2)}, u32[]{:S(2)}) collective-permute-start(f32[2,128,128]{2,1,0:T(8,128)} %convolution_add_fusion.6), channel_id=1, source_target_pairs={{12,0},{16,4},{20,8},{24,12},{28,16},{13,1},{17,5},{21,9},{25,13},... | collective-permute-start | bytes 393224 | tf_op jit(solution)/shard_map/ppermute | solution.py:380
  428.2 25.8 %collective-permute-start.18 = (f32[2,128,128]{2,1,0:T(8,128)}, f32[2,128,128]{2,1,0:T(8,128)S(1)}, u32[]{:S(2)}, u32[]{:S(2)}) collective-permute-start(f32[2,128,128]{2,1,0:T(8,128)} %convolution_add_fusion.6), channel_id=1, source_target_pairs={{4,0},{8,4},{12,8},{16,12},{20,16},{24,20},{28,24},{5,1},{9,5},{13... | collective-permute-start | bytes 393224 | tf_op jit(solution)/shard_map/ppermute | solution.py:380
  429.5 23.2 %collective-permute-start.16 = (f32[2,128,128]{2,1,0:T(8,128)}, f32[2,128,128]{2,1,0:T(8,128)S(1)}, u32[]{:S(2)}, u32[]{:S(2)}) collective-permute-start(f32[2,128,128]{2,1,0:T(8,128)} %convolution_add_fusion.6), channel_id=1, source_target_pairs={{8,0},{12,4},{16,8},{20,12},{24,16},{28,20},{9,1},{13,5},{17,9},{2... | collective-permute-start | bytes 393224 | tf_op jit(solution)/shard_map/ppermute | solution.py:380
  459.5 6.2 collective-permute-start.19
  459.6 6.4 collective-permute-start.20
  462.6 6.2 collective-permute-start.21
  499.1 6.6 collective-permute-start.22
  532.3 317.3 %reduce-scatter.6.cloned.1.call-start = ((), (), s32[]{:S(2)}) async-start(), calls=%async_computation.7 | async-start | bytes 11894784 | tf_op jit(solution)/shard_map/reduce_scatter | solution.py:611
  (40 other events, 401.9 us)
Sparse Core Ops, SparseCore 0:
  23.4 73.2 all-gather.3
  100.2 108.5 all-gather.5
  211.7 65.4 all-gather.7
  379.8 160.6 reduce-scatter.7
  542.6 152.4 reduce-scatter.3
  697.3 152.2 reduce-scatter.5

commit v2 on v1

v2 whole, which is shorter than its diff:
```python
import jax
import jax.numpy as jnp
from jax import lax
from jax.experimental import pallas as pl
from jax.experimental.pallas import tpu as pltpu
from jax.sharding import PartitionSpec as P

CONV = 4
RIM = 8
TAIL = 16
LANES = 128
BASE = 16
SEQ, FSDP = "seq", "fsdp"
BOTH = (SEQ, FSDP)
f32 = jnp.float32
bf16 = jnp.bfloat16
highest = lax.Precision.HIGHEST
NN = (((1,), (0,)), ((), ()))
NT = (((1,), (1,)), ((), ()))
TN = (((0,), (0,)), ((), ()))


class Parts:
    def __init__(self, value, passes=3):
        self.high = value.astype(bf16)
        self.low = (value - self.high.astype(f32)).astype(bf16) if passes == 3 else None


def mm(a, b, dims=NN, passes=3):
    a = a if isinstance(a, Parts) else Parts(a, passes)
    b = b if isinstance(b, Parts) else Parts(b, passes)
    if passes == 1:
        return lax.dot_general(a.high, b.high, dims, preferred_element_type=f32)
    left = jnp.concatenate([a.high, a.low, a.high], axis=dims[0][0][0])
    right = jnp.concatenate([b.high, b.high, b.low], axis=dims[0][1][0])
    return lax.dot_general(left, right, dims, preferred_element_type=f32)


def sigmoid(v):
    return 1.0 / (1.0 + jnp.exp(-v))


def iotas(rows):
    return (
        lax.broadcasted_iota(jnp.int32, (rows, rows), 0),
        lax.broadcasted_iota(jnp.int32, (rows, rows), 1),
    )


def unit_lower_inverses(lowers, rows, cols, passes):
    size = lowers[0].shape[0]
    same = (rows // BASE) == (cols // BASE)
    powers = [jnp.where(same, -lower, 0.0) for lower in lowers]
    inverses = [jnp.where(rows == cols, 1.0, power) for power in powers]
    covered = 2
    while covered < BASE:
        parts = [Parts(power, passes) for power in powers]
        powers = [mm(part, part, NN, passes) for part in parts]
        inverses = [a + mm(a, b, NN, passes) for a, b in zip(inverses, powers)]
        covered *= 2
    block = BASE
    while block < size:
        joined = ((rows // (2 * block)) == (cols // (2 * block))) & (
            (rows // block) != (cols // block)
        )
        parts = [Parts(inverse, passes) for inverse in inverses]
        inner = [
            mm(part, jnp.where(joined, lower, 0.0), NN, passes)
            for part, lower in zip(parts, lowers)
        ]
        inverses = [
            inverse - mm(off, part, NN, passes)
            for inverse, off, part in zip(inverses, inner, parts)
        ]
        block *= 2
    return inverses


def head_column(table, head):
    lanes = lax.broadcasted_iota(jnp.int32, table.shape, 1)
    first = LANES - pl.num_programs(0) * PER_STEP
    return jnp.sum(jnp.where(lanes == first + head, table, 0.0), axis=1, keepdims=True)


def load_extended(ref, scratch, rows):
    scratch[0:RIM, :] = ref[rows : rows + RIM, :].astype(f32)
    scratch[RIM : RIM + rows, :] = ref[0:rows, :].astype(f32)


def convolve(scratch, taps, rows):
    total = taps[CONV - 1 : CONV, :] * scratch[RIM : RIM + rows, :]
    for j in range(CONV - 1):
        first = RIM - (CONV - 1) + j
        total = total + taps[j : j + 1, :] * scratch[first : first + rows, :]
    return total


FRONT_PASSES = 3
PASS_PASSES = 3
BACK_PASSES = 3
PER_STEP = 2


def lanes_of(i):
    return slice(i * LANES, (i + 1) * LANES)


def front_kernel(
    pq, pk, pv, tq, tk, tv, beta_logit, q_out, k_out, v_out, t_out, pair_out, scratch
):
    rows = q_out.shape[0]
    active = []
    for ref, taps in ((pq, tq), (pk, tk), (pv, tv)):
        load_extended(ref, scratch, rows)
        c = convolve(scratch, taps, rows)
        active.append(c * sigmoid(c))
    logits = beta_logit[...]
    ri, ci = iotas(rows)
    lowers, keys, values, betas = [], [], [], []
    for i in range(PER_STEP):
        head = pl.program_id(0) * PER_STEP + i
        a, b, v = (part[:, lanes_of(i)] for part in active)
        q_out[:, lanes_of(i)] = a * lax.rsqrt(jnp.sum(a * a, axis=1, keepdims=True) + 1e-06)
        k = b * lax.rsqrt(jnp.sum(b * b, axis=1, keepdims=True) + 1e-06)
        k_out[:, lanes_of(i)] = k
        v_out[:, lanes_of(i)] = v
        beta = sigmoid(head_column(logits, head))
        part = Parts(k, FRONT_PASSES)
        lowers.append(jnp.where(ri > ci, beta * mm(part, part, NT, FRONT_PASSES), 0.0))
        keys.append(part)
        values.append(beta * v)
        betas.append(beta * k)
    inverses = unit_lower_inverses(lowers, ri, ci, FRONT_PASSES)
    for i in range(PER_STEP):
        t_out[i] = inverses[i]
        both = mm(
            inverses[i], jnp.concatenate([betas[i], values[i]], axis=1), NN, FRONT_PASSES
        )
        rs, cs = iotas(LANES)
        made = mm(both, keys[i], TN, FRONT_PASSES)
        pair_out[i, :LANES] = jnp.where(rs == cs, 1.0, 0.0) - made[:LANES]
        pair_out[i, LANES:] = made[LANES:]


def by_hop(place_ref, refs):
    count = len(refs)
    hop = lax.rem(place_ref[0] - pl.program_id(0) + count, count)
    value = refs[0][...]
    for h in range(1, count):
        value = jnp.where(hop == h, refs[h][...], value)
    return value[0]


def pass_kernel(
    place_ref, q_ref, k_ref, v_ref, t_ref, beta_logit, gate_ref, gain_ref, *rest
):
    state_refs, (branch_out, o_out, d_out, p_out) = rest[:-4], rest[-4:]
    states = by_hop(place_ref, state_refs)
    rows = q_ref.shape[0]
    logits = beta_logit[...]
    ri, ci = iotas(rows)
    for i in range(PER_STEP):
        head = pl.program_id(0) * PER_STEP + i
        cols = lanes_of(i)
        q, k, s = (Parts(m, PASS_PASSES) for m in (q_ref[:, cols], k_ref[:, cols], states[i]))
        beta = sigmoid(head_column(logits, head))
        p = jnp.where(ri >= ci, mm(q, k, NT, PASS_PASSES), 0.0)
        p_out[i] = p
        missing = v_ref[:, cols] - mm(k, s, NT, PASS_PASSES)
        d = mm(t_ref[i], beta * missing, NN, PASS_PASSES)
        d_out[:, cols] = d
        o = mm(q, s, NT, PASS_PASSES) + mm(p, d, NN, PASS_PASSES)
        o_out[:, cols] = o
        n = o * lax.rsqrt(jnp.mean(o * o, axis=1, keepdims=True) + 1e-05)
        g = gate_ref[:, cols]
        branch_out[:, cols] = (n * gain_ref[...] * (g * sigmoid(g))).astype(bf16)


def back_one_kernel(
    db_ref, o_ref, gate_ref, gain_ref, p_ref, t_ref, q_ref, k_ref, beta_logit,
    dgate_out, donorm_out, do_out, dr_out, g_out,
):
    gain = gain_ref[...]
    logits = beta_logit[...]
    for i in range(PER_STEP):
        head = pl.program_id(0) * PER_STEP + i
        cols = lanes_of(i)
        o = o_ref[:, cols]
        g = gate_ref[:, cols]
        db = db_ref[:, cols]
        beta = sigmoid(head_column(logits, head))
        scale = lax.rsqrt(jnp.mean(o * o, axis=1, keepdims=True) + 1e-05)
        n = o * scale
        sig = sigmoid(g)
        z = g * sig
        dgate_out[:, cols] = (db * n * gain * (sig * (1.0 + g * (1.0 - sig)))).astype(bf16)
        dy = db * z
        donorm_out[i] = jnp.sum(dy * n, axis=0, keepdims=True)
        dyg = dy * gain
        do = scale * dyg - o * (scale * scale * scale) * jnp.mean(dyg * o, axis=1, keepdims=True)
        do_out[:, cols] = do
        do = Parts(do, BACK_PASSES)
        dd = mm(p_ref[i], do, TN, BACK_PASSES)
        dr = mm(t_ref[i], dd, TN, BACK_PASSES)
        dr_out[:, cols] = dr
        g_out[i] = mm(do, q_ref[:, cols], TN, BACK_PASSES) - mm(
            beta * dr, k_ref[:, cols], TN, BACK_PASSES
        )


def back_two_kernel(
    place_ref, t_ref, p_ref, q_ref, k_ref, v_ref, beta_logit, do_ref, dr_ref, d_ref,
    pq, pk, pv, tq, tk, tv, *rest,
):
    count = (len(rest) - 15) // 2
    grads_in = by_hop(place_ref, rest[:count])
    states_in = by_hop(place_ref, rest[count : 2 * count])
    dq_out, dk_out, dv_out, eq_out, ek_out, ev_out, rq_out, rk_out, rv_out = rest[-15:-6]
    cq_out, ck_out, cv_out, dbeta_out, scratch, spread = rest[-6:]
    step = pl.program_id(0)
    rows = q_ref.shape[0]
    logits = beta_logit[...]
    ri, ci = iotas(rows)
    passes = BACK_PASSES

    @pl.when(step == 0)
    def _():
        dbeta_out[...] = jnp.zeros_like(dbeta_out)

    d_units = ([], [], [])
    for i in range(PER_STEP):
        head = step * PER_STEP + i
        cols = lanes_of(i)
        ds, s, q, k, do, d = (
            Parts(m, passes)
            for m in (
                grads_in[i], states_in[i], q_ref[:, cols], k_ref[:, cols], do_ref[:, cols],
                d_ref[:, cols],
            )
        )
        beta = sigmoid(head_column(logits, head))
        dr = dr_ref[:, cols] + mm(t_ref[i], mm(k, ds, NT, passes), TN, passes)
        missing = v_ref[:, cols] - mm(k, s, NT, passes)
        dp = Parts(jnp.where(ri >= ci, mm(do, d, NT, passes), 0.0), passes)
        bdr = beta * dr
        dq = mm(do, s, NN, passes) + mm(dp, k, NN, passes)
        dk = mm(dp, q, TN, passes) + mm(d, ds, NN, passes) - mm(bdr, s, NN, passes)
        da = jnp.where(ri > ci, -mm(dr, d, NT, passes), 0.0)
        dbeta = jnp.sum(dr * missing, axis=1, keepdims=True) + jnp.sum(
            da * mm(k, k, NT, passes), axis=1, keepdims=True
        )
        dm = Parts(beta * da, passes)
        dk = dk + mm(dm, k, NN, passes) + mm(dm, k, TN, passes)
        dlogit = dbeta * beta * (1.0 - beta)
        lanes = lax.broadcasted_iota(jnp.int32, dbeta_out.shape, 1)
        column = LANES - pl.num_programs(0) * PER_STEP + head
        dbeta_out[...] = jnp.where(lanes == column, dlogit, dbeta_out[...])
        for grads, grad in zip(d_units, (dq, dk, bdr)):
            grads.append(grad)

    width = q_ref.shape[1]
    spread[0:RIM, :] = jnp.zeros((RIM, width), f32)
    spread[RIM + rows : RIM + rows + RIM, :] = jnp.zeros((RIM, width), f32)
    sets = (
        (pq, tq, d_units[0], q_ref, dq_out, eq_out, rq_out, cq_out),
        (pk, tk, d_units[1], k_ref, dk_out, ek_out, rk_out, ck_out),
        (pv, tv, d_units[2], None, dv_out, ev_out, rv_out, cv_out),
    )
    for proj, taps, grads, units, out, tail_out, rim_out, tap_out in sets:
        load_extended(proj, scratch, rows)
        c = convolve(scratch, taps, rows)
        sig = sigmoid(c)
        if units is not None:
            act = c * sig
            for i in range(PER_STEP):
                cols = lanes_of(i)
                part, unit = act[:, cols], units[:, cols]
                inv = lax.rsqrt(jnp.sum(part * part, axis=1, keepdims=True) + 1e-06)
                grads[i] = (
                    grads[i] - unit * jnp.sum(unit * grads[i], axis=1, keepdims=True)
                ) * inv
        dc = jnp.concatenate(grads, axis=1) * (sig * (1.0 + c * (1.0 - sig)))
        spread[RIM : RIM + rows, :] = dc
        total = jnp.zeros((rows, width), f32)
        rim = jnp.zeros((RIM, width), f32)
        for j in range(CONV):
            lag = CONV - 1 - j
            tap = taps[j : j + 1, :]
            total = total + tap * spread[RIM + lag : RIM + lag + rows, :]
            rim = rim + tap * spread[lag : lag + RIM, :]
            first = RIM - lag
            tap_out[j : j + 1, :] = jnp.sum(
                dc * scratch[first : first + rows, :], axis=0, keepdims=True
            )
        out[...] = total.astype(bf16)
        tail_out[...] = total[rows - TAIL :]
        rim_out[...] = rim


LIGHT = pl.CostEstimate(flops=1, bytes_accessed=1, transcendentals=0)


def params():
    return pltpu.CompilerParams(
        dimension_semantics=("arbitrary",), vmem_limit_bytes=56 * 1024 * 1024
    )


def column_block(rows, heads, part):
    steps = heads // PER_STEP
    return pl.BlockSpec((rows, PER_STEP * LANES), lambda h, part=part: (0, part * steps + h))


def whole(shape):
    return pl.BlockSpec(shape, lambda h: (0,) * len(shape))


def scalar():
    return pl.BlockSpec(memory_space=pltpu.SMEM)


def per_head(shape):
    return pl.BlockSpec((PER_STEP,) + shape, lambda h: (h, 0, 0))


def pack_kernel(
    wq, wk, wv, wg, beta_ref, conv_ref, gain_ref, onorm_ref, mlp_ref, out, scratch
):
    model = wq.shape[1]
    for i, ref in enumerate((wq, wk, wv, wg)):
        out[:, i * model : (i + 1) * model] = ref[...]
    scratch[...] = jnp.zeros_like(scratch)
    taps, wide = conv_ref.shape
    scratch[0:taps, 0:wide] = conv_ref[...].astype(f32)
    for i, ref in enumerate((gain_ref, mlp_ref, onorm_ref)):
        scratch[taps + i : taps + i + 1, 0 : ref.shape[1]] = ref[...].astype(f32)
    heads = beta_ref.shape[1]
    scratch[:, LANES - heads :] = beta_ref[...].astype(f32)
    out[:, 4 * model :] = scratch[...].astype(bf16)


def run_pack(wq, wk, wv, wg, w_beta, conv, gain, onorm, mlp_gain):
    share, model = wq.shape
    return pl.pallas_call(
        pack_kernel,
        out_shape=jax.ShapeDtypeStruct((share, 4 * model + LANES), bf16),
        scratch_shapes=[pltpu.VMEM((share, LANES), f32)],
        name="pack",
    )(
        wq, wk, wv, wg, w_beta, conv, gain.reshape(1, -1), onorm.reshape(1, -1),
        mlp_gain.reshape(1, -1),
    )


def run_front(proj, taps, beta_logit, rows, heads):
    width = LANES
    p_spec = [column_block(rows + RIM, heads, i) for i in range(3)]
    t_spec = [column_block(CONV, heads, i) for i in range(3)]
    row_spec = column_block(rows, heads, 0)
    return pl.pallas_call(
        front_kernel,
        grid=(heads // PER_STEP,),
        in_specs=p_spec + t_spec + [whole((rows, LANES))],
        out_specs=[row_spec] * 3
        + [per_head((rows, rows)), per_head((2 * width, width))],
        out_shape=[jax.ShapeDtypeStruct((rows, heads * width), f32)] * 3
        + [
            jax.ShapeDtypeStruct((heads, rows, rows), f32),
            jax.ShapeDtypeStruct((heads, 2 * width, width), f32),
        ],
        scratch_shapes=[pltpu.VMEM((rows + RIM, PER_STEP * width), f32)],
        compiler_params=params(),
        cost_estimate=LIGHT,
        name="front",
    )(proj, proj, proj, taps, taps, taps, beta_logit)


def run_pass(place, q, k, v, t, beta_logit, states, gate, gain, rows, heads):
    width = LANES
    row_spec = column_block(rows, heads, 0)
    square = per_head((rows, rows))
    return pl.pallas_call(
        pass_kernel,
        grid=(heads // PER_STEP,),
        in_specs=[
            scalar(), row_spec, row_spec, row_spec, square, whole((rows, LANES)), row_spec,
            whole((1, width)),
        ]
        + [whole(state.shape) for state in states],
        out_specs=[row_spec, row_spec, row_spec, square],
        out_shape=[
            jax.ShapeDtypeStruct((rows, heads * width), bf16),
            jax.ShapeDtypeStruct((rows, heads * width), f32),
            jax.ShapeDtypeStruct((rows, heads * width), f32),
            jax.ShapeDtypeStruct((heads, rows, rows), f32),
        ],
        compiler_params=params(),
        cost_estimate=LIGHT,
        name="chunk_pass",
    )(place, q, k, v, t, beta_logit, gate, gain, *states)


def run_back_one(d_branch, o, gate, gain, p, t, q, k, beta_logit, rows, heads):
    width = LANES
    row_spec = column_block(rows, heads, 0)
    square = per_head((rows, rows))
    return pl.pallas_call(
        back_one_kernel,
        grid=(heads // PER_STEP,),
        in_specs=[
            row_spec, row_spec, row_spec, whole((1, width)), square, square, row_spec, row_spec,
            whole((rows, LANES)),
        ],
        out_specs=[row_spec, per_head((1, width)), row_spec, row_spec, per_head((width, width))],
        out_shape=[
            jax.ShapeDtypeStruct((rows, heads * width), bf16),
            jax.ShapeDtypeStruct((heads, 1, width), f32),
            jax.ShapeDtypeStruct((rows, heads * width), f32),
            jax.ShapeDtypeStruct((rows, heads * width), f32),
            jax.ShapeDtypeStruct((heads, width, width), f32),
        ],
        compiler_params=params(),
        cost_estimate=LIGHT,
        name="back_one",
    )(d_branch, o, gate, gain, p, t, q, k, beta_logit)


def run_back_two(
    place, grads, states, t, p, q, k, v, beta_logit, do, dr, d, proj, taps, rows, heads
):
    width = LANES
    row_spec = column_block(rows, heads, 0)
    square = per_head((rows, rows))
    p_spec = [column_block(rows + RIM, heads, i) for i in range(3)]
    t_spec = [column_block(CONV, heads, i) for i in range(3)]
    return pl.pallas_call(
        back_two_kernel,
        grid=(heads // PER_STEP,),
        in_specs=[
            scalar(), square, square, row_spec, row_spec, row_spec, whole((rows, LANES)),
            row_spec, row_spec, row_spec,
        ]
        + p_spec
        + t_spec
        + [whole(part.shape) for part in grads]
        + [whole(part.shape) for part in states],
        out_specs=[row_spec] * 3
        + [column_block(TAIL, heads, 0)] * 3
        + [column_block(RIM, heads, 0)] * 3
        + [column_block(CONV, heads, 0)] * 3
        + [whole((rows, LANES))],
        out_shape=[jax.ShapeDtypeStruct((rows, heads * width), bf16)] * 3
        + [jax.ShapeDtypeStruct((TAIL, heads * width), f32)] * 3
        + [jax.ShapeDtypeStruct((RIM, heads * width), f32)] * 3
        + [jax.ShapeDtypeStruct((CONV, heads * width), f32)] * 3
        + [jax.ShapeDtypeStruct((rows, LANES), f32)],
        scratch_shapes=[
            pltpu.VMEM((rows + RIM, PER_STEP * width), f32),
            pltpu.VMEM((rows + 2 * RIM, PER_STEP * width), f32),
        ],
        compiler_params=params(),
        cost_estimate=LIGHT,
        name="back_two",
    )(
        place, t, p, q, k, v, beta_logit, do, dr, d, proj, proj, proj, taps, taps, taps,
        *grads, *states,
    )


def prefix_kernel(place_ref, *rest):
    prefix_out, linear_out, ordered_ref = rest[-3:]
    parts = rest[:-3]
    count = len(parts)
    for hop in range(count):
        ordered_ref[lax.rem(place_ref[0] - hop + count, count)] = parts[hop][0]
    for m in range(ordered_ref.shape[1]):
        joined = ordered_ref[0, m]
        prefix_out[0, m] = joined
        linear_out[0, m] = joined[:LANES]
        for i in range(1, count):
            linear = ordered_ref[i, m, :LANES]
            linear_out[i, m] = linear
            joined = mm(joined, linear)
            joined = jnp.concatenate(
                [joined[:LANES], joined[LANES:] + ordered_ref[i, m, LANES:]], axis=0
            )
            prefix_out[i, m] = joined


def entry_kernel(before_ref, prefix, *rest):
    totals, out = rest[:-1], rest[-1]
    for m in range(prefix.shape[1]):
        state = jnp.zeros((LANES, LANES), f32)
        for hop in range(len(totals), 0, -1):
            total = totals[hop - 1]
            state = mm(state, total[m, :LANES]) + total[m, LANES:]
            state = jnp.where(hop <= before_ref[0], state, 0.0)
        out[0, m] = state
        for i in range(1, prefix.shape[0]):
            out[i, m] = mm(state, prefix[i - 1, m, :LANES]) + prefix[i - 1, m, LANES:]


def suffix_kernel(place_ref, linears, *rest):
    inner_out, group_out, ordered_ref = rest[-3:]
    parts = rest[:-3]
    count = len(parts)
    for hop in range(count):
        ordered_ref[lax.rem(place_ref[0] - hop + count, count)] = parts[hop][0]
    for m in range(ordered_ref.shape[1]):
        grad = jnp.zeros((LANES, LANES), f32)
        for i in range(count - 1, -1, -1):
            inner_out[i, m] = grad
            grad = mm(grad, linears[i, m], NT) + ordered_ref[i, m]
        group_out[m] = grad


def leave_kernel(after_ref, inner, linears, *rest):
    out = rest[-1]
    reach = (len(rest) - 1) // 2
    count = inner.shape[0]
    for m in range(inner.shape[1]):
        grad = jnp.zeros((LANES, LANES), f32)
        for hop in range(reach, 0, -1):
            grad = mm(grad, rest[reach + hop - 1][m], NT) + rest[hop - 1][m]
            grad = jnp.where(hop <= after_ref[0], grad, 0.0)
        for i in range(count - 1, -1, -1):
            out[i, m] = inner[i, m] + grad
            if i:
                grad = mm(grad, linears[i, m], NT)


def run_small(kernel, number, arrays, shapes, scratch, name):
    return pl.pallas_call(
        kernel,
        in_specs=[scalar()] + [pl.BlockSpec(memory_space=pltpu.VMEM)] * len(arrays),
        out_specs=[pl.BlockSpec(memory_space=pltpu.VMEM)] * len(shapes),
        out_shape=[jax.ShapeDtypeStruct(shape, f32) for shape in shapes],
        scratch_shapes=scratch,
        compiler_params=pltpu.CompilerParams(vmem_limit_bytes=56 * 1024 * 1024),
        cost_estimate=LIGHT,
        name=name,
    )(number, *arrays)


def swapped(parts, axis):
    count = lax.axis_size(axis)
    place = lax.axis_index(axis)
    result = [lax.dynamic_slice_in_dim(parts, place, 1, 0)]
    for hop in range(1, count):
        sent = lax.dynamic_slice_in_dim(parts, lax.rem(place + hop, count), 1, 0)
        result.append(lax.ppermute(sent, axis, [(i, (i + hop) % count) for i in range(count)]))
    return result


def shift_groups(array, by):
    size = lax.axis_size(SEQ)
    return lax.ppermute(
        array, SEQ, [(i, i + by) for i in range(size) if 0 <= i + by < size]
    )


def joined_chunks(pair, place):
    count = lax.axis_size(FSDP)
    heads, tall, width = pair.shape
    mine = heads // count
    parts = swapped(pair.reshape(count, mine, tall, width), FSDP)
    prefix, linears = run_small(
        prefix_kernel, place, parts,
        [(count, mine, tall, width), (count, mine, width, width)],
        [pltpu.VMEM((count, mine, tall, width), f32)], "prefix",
    )
    return prefix, linears


def states_entering(prefix, before, reach, others):
    count, mine, tall, width = prefix.shape
    group = prefix[count - 1]
    earlier = [shift_groups(group, hop) for hop in range(1, reach + 1)]
    earlier, others = tied(earlier, others)
    (entries,) = run_small(
        entry_kernel, before, [prefix] + earlier, [(count, mine, width, width)], [], "entry"
    )
    later = [shift_groups(group[:, :width], -hop) for hop in range(1, reach + 1)]
    return swapped(entries, FSDP), later, others


def state_grads_leaving(grads, linears, later, place, after, reach):
    count = lax.axis_size(FSDP)
    heads, width = grads.shape[0], grads.shape[1]
    mine = heads // count
    parts = swapped(grads.reshape(count, mine, width, width), FSDP)
    inner, group = run_small(
        suffix_kernel, place, [linears] + parts,
        [(count, mine, width, width), (mine, width, width)],
        [pltpu.VMEM((count, mine, width, width), f32)], "suffix",
    )
    beyond = [shift_groups(group, -hop) for hop in range(1, reach + 1)]
    (entries,) = run_small(
        leave_kernel, after, [inner, linears] + beyond + later,
        [(count, mine, width, width)], [], "leave",
    )
    return swapped(entries, FSDP)


def rms(values):
    return lax.rsqrt(jnp.mean(values * values, axis=-1, keepdims=True) + 1e-05)


def rms_back(values, scale, gain, dy):
    dyg = dy * gain
    grad = scale * dyg - values * (scale * scale * scale) * jnp.mean(
        dyg * values, axis=-1, keepdims=True
    )
    return grad, jnp.sum(dy * values * scale, axis=0)


def dot(a, b):
    return jnp.dot(a, b, preferred_element_type=f32)


def dot_t(a, b):
    return lax.dot_general(a, b, NT, preferred_element_type=f32)


def t_dot(a, b):
    return lax.dot_general(a, b, TN, preferred_element_type=f32)


def flips(bit, count):
    return [(i, i ^ bit) for i in range(count)]


def exchanged(array, bit):
    return lax.ppermute(array, BOTH, flips(bit, lax.axis_size(BOTH)))


def place_bits():
    index = lax.axis_index(BOTH)
    return {bit: lax.rem(index // bit, 2) for bit in (1, 2, 4)}


def tied(*values):
    return lax.optimization_barrier(values)


def owner_order(array, axis):
    count = lax.axis_size(BOTH)
    shape = array.shape
    blocks = array.reshape(shape[:axis] + (count // 8, 2, 2, 2, -1) + shape[axis + 1 :])
    order = tuple(range(axis)) + tuple(axis + i for i in (3, 2, 1, 0, 4))
    return blocks.transpose(order + tuple(range(axis + 5, blocks.ndim))).reshape(shape)


def owner_matrix(size):
    source = owner_order(jnp.arange(size, dtype=jnp.int32), 0)
    return (jnp.arange(size, dtype=jnp.int32)[:, None] == source[None, :]).astype(bf16)


def half(array, which, axis=0):
    size = array.shape[axis] // 2
    return lax.dynamic_slice_in_dim(array, which * size, size, axis)


FIRST = (2, 4)


def pick(array, axis, which):
    return lax.dynamic_index_in_dim(array, which, axis, False)


def columns(array, i):
    wide = array.shape[-1] // 2
    return array[..., i * wide : (i + 1) * wide]


def begin_terms(left, right):
    sent = t_dot(half(left, 1 - place_bits()[1], 1), right).astype(bf16)
    return exchanged(sent, 1)


def middle_terms(left, right, got):
    bits = place_bits()
    rows = left.shape[0]
    left = half(left, bits[1], 1).reshape(rows, 2, 2, -1)
    got = got.reshape((2, 2, -1) + got.shape[1:])
    kepts, sents = [], []
    for i, first in enumerate(FIRST):
        for side, outs in ((1 - bits[first], sents), (bits[first], kepts)):
            term = t_dot(pick(left, i + 1, side).reshape(rows, -1), columns(right, i))
            came = pick(columns(got, i), i, side)
            outs.append((term + came.reshape(term.shape).astype(f32)).astype(bf16))
    return kepts, sents


def cross(sents, bits):
    return [exchanged(sent, bit) for sent, bit in zip(sents, bits)]


def end_terms(kepts, gots):
    bits = place_bits()
    kepts = [(k.astype(f32) + g.astype(f32)).astype(bf16) for k, g in zip(kepts, gots)]
    mine = [half(k, bits[6 - first]) for k, first in zip(kepts, FIRST)]
    sents = [half(k, 1 - bits[6 - first]) for k, first in zip(kepts, FIRST)]
    return mine, sents


def owner_blocks(mine, gots):
    length = lax.axis_size(BOTH) // 8
    parts = [(m.astype(f32) + g.astype(f32)).astype(bf16) for m, g in zip(mine, gots)]
    return jnp.concatenate([p.reshape(length, -1, p.shape[-1]) for p in parts], axis=-1)


def stacked(blocks):
    length = len(blocks)
    place = lax.axis_index(BOTH) // 8
    back = jnp.stack(blocks[::-1] + blocks[::-1])
    return lax.dynamic_slice_in_dim(back, length - 1 - place, length, 0)


def merged(blocks, got, bit):
    mine = place_bits()[bit] == 0
    return jnp.stack([jnp.where(mine, blocks, got), jnp.where(mine, got, blocks)])


def along_last(by):
    count = lax.axis_size(BOTH)
    return [(i, (i + 8 * by) % count) for i in range(count)]


def send_blocks(blocks):
    length = blocks.shape[0]
    place = lax.axis_index(BOTH) // 8

    def block(i):
        return lax.dynamic_index_in_dim(blocks, lax.rem(i, length), 0, False)

    return [block(place)] + [
        lax.ppermute(block(place + hop), BOTH, along_last(hop)) for hop in range(1, length)
    ]


def added(parts):
    total = parts[0].astype(f32)
    for part in parts[1:]:
        total = total + part.astype(f32)
    return total


def local(
    tokens, attn_gain, w_query, w_key, w_value, conv_weight, w_beta, w_gate_out, onorm_gain,
    w_out, mlp_gain, w_mlp_gate, w_mlp_up, w_down, seq_lengths, cotangent,
):
    rows, model = tokens.shape
    heads = w_beta.shape[1]
    hidden_size = w_mlp_gate.shape[1]
    devices = lax.axis_size(BOTH)
    share = model // devices
    groups = lax.axis_size(SEQ)
    reach = groups // 2 - 1
    width = model // heads
    chan = 3 * model
    wide = chan // devices
    own_gain = onorm_gain.shape[0]
    pack_one = run_pack(
        w_query, w_key, w_value, w_gate_out, w_beta, conv_weight, attn_gain, onorm_gain, mlp_gain
    )
    full_one = lax.all_gather(pack_one, BOTH, axis=0, tiled=True)
    seq_lengths, w_mlp_gate, w_mlp_up, w_out, w_down, tokens, pack_one = (
        lax.optimization_barrier(
            (seq_lengths, w_mlp_gate, w_mlp_up, w_out, w_down, tokens, pack_one)
        )
    )
    down = [w_down] + [
        lax.ppermute(w_down, BOTH, along_last(hop)) for hop in range(1, devices // 8)
    ]
    down = stacked(down)
    halves = [columns(down, i) for i in range(2)]
    gots = cross(halves, FIRST[::-1])
    halves = [merged(h, g, bit) for h, g, bit in zip(halves, gots, FIRST[::-1])]
    full_one, halves = tied(full_one, halves)
    full_two = lax.all_gather(
        jnp.concatenate([w_out, owner_order(w_mlp_gate, 1), owner_order(w_mlp_up, 1)], axis=1),
        BOTH,
        axis=0,
        tiled=True,
    )
    to_order = owner_matrix(model)

    group_rows = rows * lax.axis_size(FSDP)
    first = lax.axis_index(BOTH) * rows
    group_first = lax.axis_index(SEQ) * group_rows
    ends = jnp.cumsum(seq_lengths)
    starts = ends - seq_lengths
    begin = jnp.max(jnp.where(starts <= first, starts, 0))
    end = jnp.min(jnp.where(ends > first, ends, rows * devices))
    opens = first == begin
    before = ((group_first - begin) // group_rows).reshape(1)
    beyond = ((end - group_first) // group_rows - 1).reshape(1)
    place = lax.axis_index(FSDP).reshape(1)

    heads_wide = chan + model
    w_heads = full_one[:, :heads_wide]
    full_misc = full_one[:, heads_wide:]
    w_out_full = full_two[:, :model]
    w_both = full_two[:, model:]
    misc = full_misc.reshape(devices, share, LANES)
    gain_one = misc[:, CONV, :share].reshape(model).astype(f32)
    gain_two = misc[:, CONV + 1, :share].reshape(model).astype(f32)
    onorm = misc[:, CONV + 2, :own_gain].reshape(1, width).astype(f32)
    taps = misc[:, :CONV, :wide].swapaxes(0, 1).reshape(CONV, chan).astype(f32)
    beta_cols = jnp.where(
        lax.broadcasted_iota(jnp.int32, full_misc.shape, 1) >= LANES - heads, full_misc, 0
    )

    rim_tokens = lax.ppermute(
        tokens[rows - RIM :], BOTH, [(i, i + 1) for i in range(devices - 1)]
    )
    rim_tokens = jnp.where(opens, jnp.zeros_like(rim_tokens), rim_tokens)
    x_all = jnp.concatenate([tokens, rim_tokens], axis=0).astype(f32)
    scale_all = rms(x_all)
    normed_all = (x_all * scale_all * gain_one).astype(bf16)
    projected = dot(normed_all, w_heads[:, :chan]).astype(bf16)
    normed = normed_all[:rows]
    x = tokens.astype(f32)
    scale_one = scale_all[:rows]
    beta_logit = dot(normed, full_misc)
    normed_order = dot(normed, to_order).astype(bf16)
    gots = cross(halves, FIRST)
    q, k, v, t, pair = run_front(projected, taps, beta_logit, rows, heads)
    pair, gots = tied(pair, gots)
    prefix, linears = joined_chunks(pair, place)
    halves = [merged(h, g, bit) for h, g, bit in zip(halves, gots, FIRST)]
    gots = cross(halves, (1, 1))
    prefix, gots = tied(prefix, gots)
    halves = [merged(h, g, 1) for h, g in zip(halves, gots)]
    halves[1] = halves[1].swapaxes(1, 2)
    full_down = jnp.concatenate([h.reshape(hidden_size, -1) for h in halves], axis=1)
    gate_logit = dot(normed, w_heads[:, chan:])
    states, later, (full_down, gate_logit) = states_entering(
        prefix, before, reach, (full_down, gate_logit)
    )
    branch, o, d, p = run_pass(
        place, q, k, v, t, beta_logit, states, gate_logit, onorm, rows, heads
    )
    hidden = x + dot(branch, w_out_full)
    scale_two = rms(hidden)
    normed_two = (hidden * scale_two * gain_two).astype(bf16)
    both_rows = dot(normed_two, w_both)
    gate_rows, up_rows = both_rows[:, :hidden_size], both_rows[:, hidden_size:]
    sig = sigmoid(gate_rows)
    act = gate_rows * sig
    inner = (act * up_rows).astype(bf16)
    down_got = begin_terms(inner, cotangent)
    output = (hidden + dot(inner, full_down)).astype(bf16)
    d_inner = dot_t(cotangent, full_down)
    d_both = jnp.concatenate(
        [d_inner * up_rows * (sig * (1.0 + gate_rows * (1.0 - sig))), d_inner * act], axis=1
    ).astype(bf16)
    grad_both = t_dot(normed_two, d_both).astype(bf16)
    down_kepts, down_sents = middle_terms(inner, cotangent, down_got)
    grad_both, d_both, down_kepts, down_sents = tied(grad_both, d_both, down_kepts, down_sents)
    g_mlp = lax.psum_scatter(grad_both, BOTH, scatter_dimension=0, tiled=True).astype(f32)
    down_gots = cross(down_sents, FIRST)
    d_normed_two = dot_t(d_both, w_both)
    d_norm, grad_gain_two = rms_back(hidden, scale_two, gain_two, d_normed_two)
    d_hidden = cotangent.astype(f32) + d_norm
    d_attn = d_hidden.astype(bf16)
    d_branch = dot_t(d_attn, w_out_full)
    branch_order = dot(branch, to_order).astype(bf16)
    out_got = begin_terms(branch_order, d_attn)
    d_branch, down_gots = tied(d_branch, down_gots)
    down_mine, down_sents = end_terms(down_kepts, down_gots)
    d_branch, down_mine, down_sents = tied(d_branch, down_mine, down_sents)
    down_gots = cross(down_sents, FIRST[::-1])
    d_gate_logit, d_onorm, d_o, d_r, state_grad = run_back_one(
        d_branch, o, gate_logit, onorm, p, t, q, k, beta_logit, rows, heads
    )
    leaving = state_grads_leaving(state_grad, linears, later, place, beyond, reach)
    out_kepts, out_sents = middle_terms(branch_order, d_attn, out_got)
    down_blocks = owner_blocks(down_mine, down_gots)
    leaving, out_kepts, out_sents, down_blocks = tied(leaving, out_kepts, out_sents, down_blocks)
    out_gots = cross(out_sents, FIRST)
    down_parts = send_blocks(down_blocks)
    outs = run_back_two(
        place, leaving, states, t, p, q, k, v, beta_logit, d_o, d_r, d, projected, taps,
        rows, heads,
    )
    outs, out_gots = tied(outs, out_gots)
    tails = jnp.concatenate(outs[3:6], axis=1)
    rims = jnp.concatenate(outs[6:9], axis=1)
    d_beta = outs[12].astype(bf16)
    rims = jnp.where(opens, jnp.zeros_like(rims), rims)
    rims = lax.ppermute(rims, BOTH, [(i + 1, i) for i in range(devices - 1)])
    tails = tails + jnp.pad(rims, ((TAIL - RIM, 0), (0, 0)))
    d_proj = lax.dynamic_update_slice_in_dim(
        jnp.concatenate(outs[0:3], axis=1), tails.astype(bf16), rows - TAIL, 0
    )
    d_heads = jnp.concatenate([d_proj, d_gate_logit], axis=1)
    d_heads, d_beta, out_gots = tied(d_heads, d_beta, out_gots)
    last_got = begin_terms(normed_order, d_heads)
    d_normed = dot_t(d_heads, w_heads) + dot_t(d_beta, beta_cols)
    d_token_norm, grad_gain_one = rms_back(x, scale_one, gain_one, d_normed)
    grad_tokens = d_hidden + d_token_norm
    out_mine, out_sents = end_terms(out_kepts, out_gots)
    last_got, grad_tokens, grad_gain_one, out_mine, out_sents = tied(
        last_got, grad_tokens, grad_gain_one, out_mine, out_sents
    )
    last_kepts, last_sents = middle_terms(normed_order, d_heads, last_got)
    last_kepts, last_sents, out_mine, out_sents, down_parts, grad_gain_one, d_beta = tied(
        last_kepts, last_sents, out_mine, out_sents, down_parts, grad_gain_one, d_beta
    )
    last_gots = cross(last_sents, FIRST)
    out_gots = cross(out_sents, FIRST[::-1])
    grad_beta = t_dot(d_beta, normed)[LANES - heads :]
    table = jnp.concatenate(
        list(outs[9:12])
        + [
            grad_gain_one.reshape(1, model),
            grad_gain_two.reshape(1, model),
            jnp.pad(jnp.sum(d_onorm, axis=(0, 1)).reshape(1, width), ((0, 0), (0, model - width))),
            grad_beta,
        ],
        axis=0,
    )
    tables = [table] + [
        lax.ppermute(table, BOTH, along_last(hop)) for hop in range(1, devices // 8)
    ]
    last_gots, out_gots, tables = tied(last_gots, out_gots, tables)
    last_mine, last_sents = end_terms(last_kepts, last_gots)
    last_mine, last_sents, out_mine, out_gots, tables, g_mlp, down_parts = tied(
        last_mine, last_sents, out_mine, out_gots, tables, g_mlp, down_parts
    )
    last_gots = cross(last_sents, FIRST[::-1])
    table = added(tables)
    table_got = exchanged(table, 1)
    last_gots, table, table_got = tied(last_gots, table, table_got)
    last_parts = send_blocks(
        jnp.concatenate(
            [owner_blocks(last_mine, last_gots), owner_blocks(out_mine, out_gots)], axis=-1
        )
    )
    table = table + table_got
    for bit in (4, 2):
        table = table + exchanged(table, bit)
    g_down = added(down_parts)
    g_last = added(last_parts)
    index = lax.axis_index(BOTH)
    g_taps = jnp.concatenate([table[i * CONV : (i + 1) * CONV] for i in range(3)], axis=1)

    def own(rows_of, size):
        return lax.dynamic_slice_in_dim(rows_of, index * size, size, rows_of.ndim - 1)

    line = 3 * CONV

    def from_order(grad):
        blocks = grad.reshape(share, 2, 2, 2, devices // 8, -1)
        return blocks.transpose(0, 4, 3, 2, 1, 5).reshape(share, hidden_size)

    return (
        output,
        grad_tokens,
        own(table[line], share),
        g_last[:, :model],
        g_last[:, model : 2 * model],
        g_last[:, 2 * model : chan],
        own(g_taps, wide),
        own(table[line + 3 :], share).T,
        g_last[:, chan : chan + model],
        own(table[line + 2], own_gain),
        g_last[:, heads_wide:],
        own(table[line + 1], share),
        from_order(g_mlp[:, :hidden_size]),
        from_order(g_mlp[:, hidden_size:]),
        g_down,
    )


def solution(mesh):
    rows = P(BOTH, None)
    flat = P(BOTH)
    cols = P(None, BOTH)
    return jax.shard_map(
        local,
        mesh=mesh,
        in_specs=(
            rows, flat, rows, rows, rows, cols, rows, rows, flat, rows, flat, rows, rows, rows,
            P(), rows,
        ),
        out_specs=(
            rows, rows, flat, rows, rows, rows, cols, rows, rows, flat, rows, flat, rows, rows,
            rows,
        ),
        check_vma=False,
    )
```

time: 868 us -> 565 us (0.65)
  waiting for transfers between devices: 516 us -> 190 us
  starting transfers between devices: 33.3 us -> 106 us
  Pallas kernels: 123 us -> 79.1 us
  local copies, waits for them, and re-layouts: 31.8 us -> 57.4 us
  matrix products: 92.2 us -> 74.8 us
  other arithmetic: 45 us -> 30.4 us
    reduce_scatter x3 -> x1, waiting for transfers between devices: 287 us -> 0.01 us  [local(): lax.psum_scatter(grad_both, BOTH, scatter_dimension=0, tiled=True)]
    all_gather x2 -> x1, waiting for transfers between devices: 112 us -> 0.02 us  [local(): lax.all_gather(jnp.concatenate([w_out, owner_order(w_mlp_gate, 1), owner_...]
    ppermute x12 -> x48, starting transfers between devices: 12.2 us -> 85.9 us  [the longest x24 47.5 us: exchanged(): return lax.ppermute(array, BOTH, flips(bit, lax.axis_size(BOTH)))]
    ppermute x12 -> x48, waiting for transfers between devices: 20.9 us -> 94.6 us  [the longest x24 26.9 us: exchanged(): return lax.ppermute(array, BOTH, flips(bit, lax.axis_size(BOTH)))]
    pallas_call x4 -> x9, Pallas kernels: 123 us -> 79.1 us  [the longest x1 23.7 us: run_front(): pl.pallas_call(front_kernel, grid=(heads // PER_STEP,), in_specs=p_spec +...]
    dynamic_slice x4 -> x31, local copies, waits for them, and re-layouts: 0.91 us -> 28.3 us  [the longest x12 12 us: half(): return lax.dynamic_slice_in_dim(array, which * size, size, axis)]
    all_gather x1, waiting for transfers between devices: 71.5 us -> 45.6 us  [local(): full_one = lax.all_gather(pack_one, BOTH, axis=0, tiled=True)]
    ppermute x9, waiting for transfers between devices: 24.1 us -> 49.6 us  [shift_groups(): lax.ppermute(array, SEQ, [(i, i + by) for i in range(size) if 0 <= i + by...]
  transfers between devices with their start and end apart: 29 -> 62, of which waited for: 18 -> 30; matrix products, arithmetic and copies ran while one was open for 17% -> 24% of each run, Pallas kernels for 14% -> 14%
where the time goes in v2:
time: 565 us; the launch traced here: 555 us
  waiting for transfers between devices  190 us (34%)
  starting transfers between devices  106 us (19%)
  Pallas kernels  79.1 us (14%)
  matrix products  74.8 us (13%)
  local copies, waits for them, and re-layouts  57.4 us (10%)
  other arithmetic  30.4 us (5%)
  between operations  17.9 us (3%)
    ppermute x9, waiting for transfers between devices, shift_groups(): lax.ppermute(array, SEQ, [(i, i + by) for i in range(size) if 0 <= i + by...  49.6 us
    ppermute x24, starting transfers between devices, exchanged(): return lax.ppermute(array, BOTH, flips(bit, lax.axis_size(BOTH)))  47.5 us
    all_gather x1, waiting for transfers between devices, local(): full_one = lax.all_gather(pack_one, BOTH, axis=0, tiled=True)  45.6 us
    dot_general x8, matrix products, dot(): return jnp.dot(a, b, preferred_element_type=f32)  28.2 us
    ppermute x24, waiting for transfers between devices, exchanged(): return lax.ppermute(array, BOTH, flips(bit, lax.axis_size(BOTH)))  26.9 us
    ppermute x12, waiting for transfers between devices, swapped(): lax.ppermute(sent, axis, [(i, (i + hop) % count) for i in range(count)])  24.9 us
    dot_general x17, matrix products, t_dot(): return lax.dot_general(a, b, TN, preferred_element_type=f32)  24.5 us
    pallas_call x1, Pallas kernels, run_front(): pl.pallas_call(front_kernel, grid=(heads // PER_STEP,), in_specs=p_spec +...  23.7 us
  transfers between devices with their start and end apart: 62, of which 30 were waited for; matrix products, arithmetic and copies ran while one was open for 24% of the time, Pallas kernels for 14%

profile of v2, /device:TPU:0, one launch (start us, length us, event | category | flops | bytes accessed | tf_op | source)
XLA Modules:
  0.0 555.1 jit_solution(3352807739556312491)
XLA Ops:
  14.5 5.1 collective-permute-start.1
  25.7 14.8 %collective-permute-done.2 = bf16[88,1024]{1,0:T(8,128)(2,1)S(1)} collective-permute-done((bf16[88,1024]{1,0:T(8,128)(2,1)S(1)}, bf16[88,1024]{1,0:T(8,128)(2,1)S(1)}, u32[]{:S(2)}, u32[]{:S(2)}) %collective-permute-start.2) | collective-permute-done | bytes 180256 | tf_op jit(solution)/shard_map/ppermute | solution.py:774
  44.1 6.5 %collective-permute-done.4 = bf16[4,88,512]{2,1,0:T(8,128)(2,1)S(1)} collective-permute-done((bf16[4,88,512]{2,1,0:T(8,128)(2,1)S(1)}, bf16[4,88,512]{2,1,0:T(8,128)(2,1)S(1)}, u32[]{:S(2)}, u32[]{:S(2)}) %collective-permute-start.4) | collective-permute-done | bytes 360480 | tf_op jit(solution)/shard_map/ppermute | solution.py:634
  50.7 3.8 collective-permute-done.5
  54.7 45.6 %all-gather.3.cloned.1.call-done = bf16[1024,4224]{1,0:T(8,128)(2,1)} async-done(((bf16[32,4224]{1,0:T(8,128)(2,1)}), bf16[1024,4224]{1,0:T(8,128)(2,1)}) %all-gather.3.cloned.1.call-update) | async-done | bytes 8650768 | tf_op jit(solution)/shard_map/all_gather | solution.py:767
  106.4 5.8 %fusion.10.pq.pk.pv = bf16[264,3072]{1,0:T(8,128)(2,1)} fusion(bf16[264,1024]{1,0:T(8,128)(2,1)S(1)} %fusion.37, bf16[1024,4224]{1,0:T(8,128)(2,1)} %all-gather.3.cloned.1.call-done), kind=kOutput, calls=%fused_computation.15 | convolution fusion | flops 1661755392 | bytes 8454144 | tf_op jit(solution)/shard_map/dot_general | solution.py:618
  112.9 23.7 %front.1 = (f32[256,1024]{1,0:T(8,128)}, f32[256,1024]{1,0:T(8,128)}, f32[256,1024]{1,0:T(8,128)}, f32[8,256,256]{2,1,0:T(8,128)}, f32[8,256,128]{2,1,0:T(8,128)}) custom-call(bf16[264,3072]{1,0:T(8,128)(2,1)} %fusion.10.pq.pk.pv, bf16[264,3072]{1,0:T(8,128)(2,1)} %fusion.10.pq.pk.pv, bf16[264,3072]{1,0:T(8,128)(2,1)} %fusion.10.pq.pk.pv, ...), custom_call_target="tpu_custom_call" | custom-call | flops 1 | bytes 1 | tf_op jit(solution)/shard_map/front/pallas_call | solution.py:360
  155.2 4.0 collective-permute-done.10.rest_3_
  166.6 3.4 collective-permute-start.14
  170.0 3.8 collective-permute-start.15
  182.0 11.2 %collective-permute-done.15.rest_2_ = f32[2,256,128]{2,1,0:T(8,128)S(1)} collective-permute-done((f32[2,256,128]{2,1,0:T(8,128)S(1)}, f32[2,256,128]{2,1,0:T(8,128)S(1)}, u32[]{:S(2)}, u32[]{:S(2)}) %collective-permute-start.15) | collective-permute-done | bytes 262176 | tf_op jit(solution)/shard_map/ppermute | solution.py:557
  207.4 9.6 %chunk_pass.1 = (bf16[256,1024]{1,0:T(8,128)(2,1)}, f32[256,1024]{1,0:T(8,128)}, f32[256,1024]{1,0:T(8,128)}, f32[8,256,256]{2,1,0:T(8,128)}) custom-call(s32[1]{0:T(128)} %bitcast.3.place_ref, f32[256,1024]{1,0:T(8,128)} %get-tuple-element.162.q_ref, f32[256,1024]{1,0:T(8,128)} %get-tuple-element.163.k_ref, f32[256,1024]{1,0:T(8,128)} %get-tuple-element.164.v_ref, ...), custom_call_target="tpu_custom_call" | custom-call | flops 1 | bytes 1 | tf_op jit(solution)/shard_map/chunk_pass/pallas_call | solution.py:382
  219.8 6.5 %fusion.2 = f32[256,5632]{1,0:T(8,128)S(1)} fusion(bf16[1024,6656]{1,0:T(8,128)(2,1)} %all-gather.5.cloned.1.call-done, f32[256,1024]{1,0:T(8,128)S(1)} %get-tuple-element.409, f32[1024]{0:T(1024)S(1)} %reshape.498, f32[256]{0:T(256)S(1)} %get-tuple-element.407), kind=kOutput, calls=%fused_computation.3 | convolution fusion | flops 2953576448 | bytes 18355200 | tf_op jit(solution)/shard_map/dot_general | solution.py:618
  226.3 4.0 multiply_convert_fusion.1
  242.9 6.3 %convolution_convert_fusion = bf16[1024,5632]{1,0:T(8,128)(2,1)} fusion(f32[256,1024]{1,0:T(8,128)S(1)} %copy-done.6, f32[1024]{0:T(1024)S(1)} %reshape.498, f32[256]{0:T(256)S(1)} %get-tuple-element.407, bf16[256,2816]{1,0:T(8,128)(2,1)S(1)} %copy-done.4, bf16[256,2816]{1,0:T(8,128)(2,1)S(1)} %copy-done.3), kind=kOutput, calls=%fused_computation | convolution fusion | flops 2965110784 | bytes 15471616 | tf_op jit(solution)/shard_map/dot_general | solution.py:626
  260.2 8.9 %collective-permute-start.21 = (bf16[704,512]{1,0:T(8,128)(2,1)}, bf16[704,512]{1,0:T(8,128)(2,1)S(1)}, u32[]{:S(2)}, u32[]{:S(2)}) collective-permute-start(bf16[704,512]{1,0:T(8,128)(2,1)} %fusion.26), channel_id=1, source_target_pairs={{0,4},{1,5},{2,6},{3,7},{4,0},{5,1},{6,2},{7,3},{8,12},{9,13},{10,... | collective-permute-start | bytes 2162696 | tf_op jit(solution)/shard_map/ppermute | solution.py:634
  269.1 7.3 %multiply_reduce_fusion = (f32[1024]{0:T(1024)S(1)}, f32[256]{0:T(256)S(1)}, f32[256,1024]{1,0:T(8,128)S(1)}) fusion(f32[256,1024]{1,0:T(8,128)S(1)} %copy-done.7, f32[256]{0:T(256)S(1)} %get-tuple-element.407, f32[1024]{0:T(1024)S(1)} %reshape.498, bf16[256,5632]{1,0:T(8,128)(2,1)} %pad_maximum_fusion.3, bf16[1024,6656]{1,0:T(8,128)(2,1)} %all-gather.5.cloned.1.call-done), kind=kOutput, calls=%fused_computation.85 | convolution fusion | flops 2954361600 | bytes 16525312 | tf_op jit(solution)/shard_map/dot_general | solution.py:622
  286.6 9.2 %back_one.1 = (bf16[256,1024]{1,0:T(8,128)(2,1)}, f32[8,1,128]{2,1,0:T(1,128)}, f32[256,1024]{1,0:T(8,128)}, f32[256,1024]{1,0:T(8,128)}, f32[8,128,128]{2,1,0:T(8,128)}) custom-call(f32[256,1024]{1,0:T(8,128)} %fusion.22.db_ref, f32[256,1024]{1,0:T(8,128)} %get-tuple-element.195.o_ref, f32[256,1024]{1,0:T(8,128)} %fusion.20.gate_ref, ...), custom_call_target="tpu_custom_call" | custom-call | flops 1 | bytes 1 | tf_op jit(solution)/shard_map/back_one/pallas_call | solution.py:407
  308.1 3.7 collective-permute-done.24.rest_3_
  317.3 22.2 %collective-permute-done.29.rest_4_ = f32[2,128,128]{2,1,0:T(8,128)S(1)} collective-permute-done((f32[2,128,128]{2,1,0:T(8,128)}, f32[2,128,128]{2,1,0:T(8,128)S(1)}, u32[]{:S(2)}, u32[]{:S(2)}) %collective-permute-start.29) | collective-permute-done | bytes 131104 | tf_op jit(solution)/shard_map/ppermute | solution.py:557
  340.9 9.2 %collective-permute-done.30.rest_5_ = f32[2,128,128]{2,1,0:T(8,128)S(1)} collective-permute-done((f32[2,128,128]{2,1,0:T(8,128)}, f32[2,128,128]{2,1,0:T(8,128)S(1)}, u32[]{:S(2)}, u32[]{:S(2)}) %collective-permute-start.30) | collective-permute-done | bytes 131104 | tf_op jit(solution)/shard_map/ppermute | solution.py:557
  362.1 3.7 leave.1
  375.6 7.0 %collective-permute-done.31.rest_1_ = f32[1,2,128,128]{3,2,1,0:T(8,128)S(1)} collective-permute-done((f32[1,2,128,128]{3,2,1,0:T(8,128)S(1)}, f32[1,2,128,128]{3,2,1,0:T(8,128)S(1)}, u32[]{:S(2)}, u32[]{:S(2)}) %collective-permute-start.31) | collective-permute-done | bytes 131104 | tf_op jit(solution)/shard_map/ppermute | solution.py:551
  385.6 9.0 %collective-permute-start.38 = (bf16[256,512]{1,0:T(8,128)(2,1)S(1)}, bf16[256,512]{1,0:T(8,128)(2,1)S(1)}, u32[]{:S(2)}, u32[]{:S(2)}) collective-permute-start(bf16[256,512]{1,0:T(8,128)(2,1)S(1)} %fusion.51), channel_id=1, source_target_pairs={{0,4},{1,5},{2,6},{3,7},{4,0},{5,1},{6,2},{7,3},{8,12},{9,13},{10,... | collective-permute-start | bytes 786440 | tf_op jit(solution)/shard_map/ppermute | solution.py:634
  395.7 21.5 %back_two.1 = (bf16[256,1024]{1,0:T(8,128)(2,1)}, bf16[256,1024]{1,0:T(8,128)(2,1)}, bf16[256,1024]{1,0:T(8,128)(2,1)}, f32[16,1024]{1,0:T(8,128)}, f32[16,1024]...) custom-call(s32[1]{0:T(128)} %bitcast.3.place_ref, ...), custom_call_target="tpu_custom_call" | custom-call | flops 1 | bytes 1 | tf_op jit(solution)/shard_map/back_two/pallas_call | solution.py:436
  425.4 5.6 %collective-permute-start.40 = (bf16[512,4096]{1,0:T(8,128)(2,1)}, bf16[512,4096]{1,0:T(8,128)(2,1)}, u32[]{:S(2)}, u32[]{:S(2)}) collective-permute-start(bf16[512,4096]{1,0:T(8,128)(2,1)} %convolution_convert_fusion.1), channel_id=1, source_target_pairs={{0,1},{1,0},{2,3},{3,2},{4,5},{5,4},{6,7},{7,6},{8,9},{9,8},{10,11... | collective-permute-start | bytes 12582920 | tf_op jit(solution)/shard_map/ppermute | solution.py:634
  443.5 5.8 %fusion.4 = f32[256,1024]{1,0:T(8,128)S(1)} fusion(bf16[256,4096]{1,0:T(8,128)(2,1)S(1)} %pad_maximum_fusion.4, bf16[1024,4224]{1,0:T(8,128)(2,1)} %all-gather.3.cloned.1.call-done), kind=kOutput, calls=%fused_computation.5 | convolution fusion | flops 2147483648 | bytes 11534336 | tf_op jit(solution)/shard_map/dot_general | solution.py:622
  463.4 3.5 collective-permute-start.48
  475.2 5.8 %fusion.32 = bf16[256,1024]{1,0:T(8,128)(2,1)} fusion(f32[256,1024]{1,0:T(8,128)} %copy-done.5, bf16[256,2816]{1,0:T(8,128)(2,1)} %copy-done.18, bf16[2816,1024]{1,0:T(8,128)(2,1)} %pad_maximum_fusion), kind=kOutput, calls=%fused_computation.71 | convolution fusion | flops 1476919296 | bytes 8781824 | tf_op jit(solution)/shard_map/dot_general | solution.py:618
  481.0 8.7 %collective-permute-done.46 = bf16[128,512]{1,0:T(8,128)(2,1)S(1)} collective-permute-done((bf16[128,512]{1,0:T(8,128)(2,1)S(1)}, bf16[128,512]{1,0:T(8,128)(2,1)S(1)}, u32[]{:S(2)}, u32[]{:S(2)}) %collective-permute-start.46) | collective-permute-done | bytes 131104 | tf_op jit(solution)/shard_map/ppermute | solution.py:634
  517.1 4.2 collective-permute-start.57
  525.1 21.9 %collective-permute-done.57 = bf16[32,5120]{1,0:T(8,128)(2,1)S(1)} collective-permute-done((bf16[32,5120]{1,0:T(8,128)(2,1)S(1)}, bf16[32,5120]{1,0:T(8,128)(2,1)S(1)}, u32[]{:S(2)}, u32[]{:S(2)}) %collective-permute-start.57) | collective-permute-done | bytes 327712 | tf_op jit(solution)/shard_map/ppermute | solution.py:738
  (449 shorter events, 225.8 us)
Async XLA Ops:
  7.2 93.1 %all-gather.3.cloned.1.call-start = ((), (), s32[]{:S(2)}) async-start(), calls=%async_computation.1 | async-start | bytes 8921088 | tf_op jit(solution)/shard_map/all_gather | solution.py:767
  10.5 206.5 %all-gather.5.cloned.1.call-start = ((), (), s32[]{:S(2)}) async-start(), calls=%async_computation.2 | async-start | bytes 14057472 | tf_op jit(solution)/shard_map/all_gather | solution.py:781
  14.5 477.9 %reduce-scatter.2.cloned.1.call-start = ((), (), s32[]{:S(2)}) async-start(), calls=%async_computation.3 | async-start | bytes 11894784 | tf_op jit(solution)/shard_map/reduce_scatter | solution.py:862
  19.7 20.8 %collective-permute-start.2 = (bf16[88,1024]{1,0:T(8,128)(2,1)S(1)}, bf16[88,1024]{1,0:T(8,128)(2,1)S(1)}, u32[]{:S(2)}, u32[]{:S(2)}) collective-permute-start(bf16[88,1024]{1,0:T(8,128)(2,1)S(1)} %copy-done.25), channel_id=1, source_target_pairs={{0,16},{1,17},{2,18},{3,19},{4,20},{5,21},{6,22},{7,23},{8,24},{9,... | collective-permute-start | bytes 540680 | tf_op jit(solution)/shard_map/ppermute | solution.py:774
  19.7 20.9 %collective-permute-start.3 = (bf16[88,1024]{1,0:T(8,128)(2,1)S(1)}, bf16[88,1024]{1,0:T(8,128)(2,1)S(1)}, u32[]{:S(2)}, u32[]{:S(2)}) collective-permute-start(bf16[88,1024]{1,0:T(8,128)(2,1)S(1)} %copy-done.25), channel_id=1, source_target_pairs={{0,8},{1,9},{2,10},{3,11},{4,12},{5,13},{6,14},{7,15},{8,16},{9,17... | collective-permute-start | bytes 540680 | tf_op jit(solution)/shard_map/ppermute | solution.py:774
  20.7 21.6 %collective-permute-start = (bf16[8,1024]{1,0:T(8,128)(2,1)S(1)}, bf16[8,1024]{1,0:T(8,128)(2,1)S(1)}, u32[]{:S(2)}, u32[]{:S(2)}) collective-permute-start(bf16[8,1024]{1,0:T(8,128)(2,1)S(1)} %slice.157), channel_id=1, source_target_pairs={{0,1},{1,2},{2,3},{3,4},{4,5},{5,6},{6,7},{7,8},{8,9},{9,10},{10,1... | collective-permute-start | bytes 49160 | tf_op jit(solution)/shard_map/ppermute | solution.py:815
  102.1 34.5 %collective-permute-start.6 = (bf16[2,4,88,512]{3,2,1,0:T(8,128)(2,1)S(1)}, bf16[2,4,88,512]{3,2,1,0:T(8,128)(2,1)}, u32[]{:S(2)}, u32[]{:S(2)}) collective-permute-start(bf16[2,4,88,512]{3,2,1,0:T(8,128)(2,1)S(1)} %get-tuple-element.167), channel_id=1, source_target_pairs={{0,2},{1,3},{2,0},{3,1},{4,6},{5,7},{6,4},{7,5},{8,10},{9,11},{10,... | collective-permute-start | bytes 2162696 | tf_op jit(solution)/shard_map/ppermute | solution.py:634
  103.6 33.1 %collective-permute-start.7 = (bf16[2,4,88,512]{3,2,1,0:T(8,128)(2,1)S(1)}, bf16[2,4,88,512]{3,2,1,0:T(8,128)(2,1)S(1)}, u32[]{:S(2)}, u32[]{:S(2)}) collective-permute-start(bf16[2,4,88,512]{3,2,1,0:T(8,128)(2,1)S(1)} %get-tuple-element.168), channel_id=1, source_target_pairs={{0,4},{1,5},{2,6},{3,7},{4,0},{5,1},{6,2},{7,3},{8,12},{9,13},{10,... | collective-permute-start | bytes 2162696 | tf_op jit(solution)/shard_map/ppermute | solution.py:634
  139.4 23.9 %collective-permute-start.11 = (bf16[2,2,4,88,512]{4,3,2,0,1:T(8,128)(2,1)}, bf16[2,2,4,88,512]{4,3,2,0,1:T(8,128)(2,1)}, u32[]{:S(2)}, u32[]{:S(2)}) collective-permute-start(bf16[2,2,4,88,512]{4,3,2,0,1:T(8,128)(2,1)} %pad_maximum_fusion.6), channel_id=1, source_target_pairs={{0,1},{1,0},{2,3},{3,2},{4,5},{5,4},{6,7},{7,6},{8,9},{9,8},{10,11... | collective-permute-start | bytes 4325384 | tf_op jit(solution)/shard_map/ppermute | solution.py:634
  142.0 21.3 %collective-permute-start.12 = (bf16[2,2,4,88,512]{4,3,2,0,1:T(8,128)(2,1)}, bf16[2,2,4,88,512]{4,3,2,0,1:T(8,128)(2,1)}, u32[]{:S(2)}, u32[]{:S(2)}) collective-permute-start(bf16[2,2,4,88,512]{4,3,2,0,1:T(8,128)(2,1)} %pad_maximum_fusion.7), channel_id=1, source_target_pairs={{0,1},{1,0},{2,3},{3,2},{4,5},{5,4},{6,7},{7,6},{8,9},{9,8},{10,11... | collective-permute-start | bytes 4325384 | tf_op jit(solution)/shard_map/ppermute | solution.py:634
  170.0 23.2 %collective-permute-start.15 = (f32[2,256,128]{2,1,0:T(8,128)S(1)}, f32[2,256,128]{2,1,0:T(8,128)S(1)}, u32[]{:S(2)}, u32[]{:S(2)}) collective-permute-start(f32[2,256,128]{2,1,0:T(8,128)S(1)} %slice_bitcast_fusion), channel_id=1, source_target_pairs={{0,12},{4,16},{8,20},{12,24},{16,28},{1,13},{5,17},{9,21},{13,25},... | collective-permute-start | bytes 786440 | tf_op jit(solution)/shard_map/ppermute | solution.py:557
  258.6 24.0 %collective-permute-start.20 = (bf16[704,512]{1,0:T(8,128)(2,1)}, bf16[704,512]{1,0:T(8,128)(2,1)S(1)}, u32[]{:S(2)}, u32[]{:S(2)}) collective-permute-start(bf16[704,512]{1,0:T(8,128)(2,1)} %fusion.27), channel_id=1, source_target_pairs={{0,2},{1,3},{2,0},{3,1},{4,6},{5,7},{6,4},{7,5},{8,10},{9,11},{10,... | collective-permute-start | bytes 2162696 | tf_op jit(solution)/shard_map/ppermute | solution.py:634
  260.2 25.2 %collective-permute-start.21 = (bf16[704,512]{1,0:T(8,128)(2,1)}, bf16[704,512]{1,0:T(8,128)(2,1)S(1)}, u32[]{:S(2)}, u32[]{:S(2)}) collective-permute-start(bf16[704,512]{1,0:T(8,128)(2,1)} %fusion.26), channel_id=1, source_target_pairs={{0,4},{1,5},{2,6},{3,7},{4,0},{5,1},{6,2},{7,3},{8,12},{9,13},{10,... | collective-permute-start | bytes 2162696 | tf_op jit(solution)/shard_map/ppermute | solution.py:634
  279.2 92.2 %collective-permute-start.34 = (bf16[512,1024]{1,0:T(8,128)(2,1)}, bf16[512,1024]{1,0:T(8,128)(2,1)}, u32[]{:S(2)}, u32[]{:S(2)}) collective-permute-start(bf16[512,1024]{1,0:T(8,128)(2,1)} %convolution_convert_fusion.3), channel_id=1, source_target_pairs={{0,1},{1,0},{2,3},{3,2},{4,5},{5,4},{6,7},{7,6},{8,9},{9,8},{10,11... | collective-permute-start | bytes 3145736 | tf_op jit(solution)/shard_map/ppermute | solution.py:634
  304.6 34.9 %collective-permute-start.29 = (f32[2,128,128]{2,1,0:T(8,128)}, f32[2,128,128]{2,1,0:T(8,128)S(1)}, u32[]{:S(2)}, u32[]{:S(2)}) collective-permute-start(f32[2,128,128]{2,1,0:T(8,128)} %slice.216), channel_id=1, source_target_pairs={{8,0},{12,4},{16,8},{20,12},{24,16},{28,20},{9,1},{13,5},{17,9},{2... | collective-permute-start | bytes 393224 | tf_op jit(solution)/shard_map/ppermute | solution.py:557
  306.8 43.3 %collective-permute-start.30 = (f32[2,128,128]{2,1,0:T(8,128)}, f32[2,128,128]{2,1,0:T(8,128)S(1)}, u32[]{:S(2)}, u32[]{:S(2)}) collective-permute-start(f32[2,128,128]{2,1,0:T(8,128)} %slice.216), channel_id=1, source_target_pairs={{12,0},{16,4},{20,8},{24,12},{28,16},{13,1},{17,5},{21,9},{25,13},... | collective-permute-start | bytes 393224 | tf_op jit(solution)/shard_map/ppermute | solution.py:557
  314.7 37.9 %collective-permute-start.25 = (f32[2,128,128]{2,1,0:T(8,128)}, f32[2,128,128]{2,1,0:T(8,128)S(1)}, u32[]{:S(2)}, u32[]{:S(2)}) collective-permute-start(f32[2,128,128]{2,1,0:T(8,128)} %get-tuple-element.202), channel_id=1, source_target_pairs={{4,0},{8,4},{12,8},{16,12},{20,16},{24,20},{28,24},{5,1},{9,5},{13... | collective-permute-start | bytes 393224 | tf_op jit(solution)/shard_map/ppermute | solution.py:557
  316.0 42.3 %collective-permute-start.26 = (f32[2,128,128]{2,1,0:T(8,128)}, f32[2,128,128]{2,1,0:T(8,128)S(1)}, u32[]{:S(2)}, u32[]{:S(2)}) collective-permute-start(f32[2,128,128]{2,1,0:T(8,128)} %get-tuple-element.202), channel_id=1, source_target_pairs={{8,0},{12,4},{16,8},{20,12},{24,16},{28,20},{9,1},{13,5},{17,9},{2... | collective-permute-start | bytes 393224 | tf_op jit(solution)/shard_map/ppermute | solution.py:557
  339.6 21.9 %collective-permute-start.27 = (f32[2,128,128]{2,1,0:T(8,128)}, f32[2,128,128]{2,1,0:T(8,128)S(1)}, u32[]{:S(2)}, u32[]{:S(2)}) collective-permute-start(f32[2,128,128]{2,1,0:T(8,128)} %get-tuple-element.202), channel_id=1, source_target_pairs={{12,0},{16,4},{20,8},{24,12},{28,16},{13,1},{17,5},{21,9},{25,13},... | collective-permute-start | bytes 393224 | tf_op jit(solution)/shard_map/ppermute | solution.py:557
  350.1 25.1 %collective-permute-start.36 = (bf16[352,512]{1,0:T(8,128)(2,1)}, bf16[352,512]{1,0:T(8,128)(2,1)S(1)}, u32[]{:S(2)}, u32[]{:S(2)}) collective-permute-start(bf16[352,512]{1,0:T(8,128)(2,1)} %get-tuple-element.206), channel_id=1, source_target_pairs={{0,2},{1,3},{2,0},{3,1},{4,6},{5,7},{6,4},{7,5},{8,10},{9,11},{10,... | collective-permute-start | bytes 1081352 | tf_op jit(solution)/shard_map/ppermute | solution.py:634
  352.6 22.7 %collective-permute-start.35 = (bf16[352,512]{1,0:T(8,128)(2,1)S(1)}, bf16[352,512]{1,0:T(8,128)(2,1)S(1)}, u32[]{:S(2)}, u32[]{:S(2)}) collective-permute-start(bf16[352,512]{1,0:T(8,128)(2,1)S(1)} %get-tuple-element.204), channel_id=1, source_target_pairs={{0,4},{1,5},{2,6},{3,7},{4,0},{5,1},{6,2},{7,3},{8,12},{9,13},{10,... | collective-permute-start | bytes 1081352 | tf_op jit(solution)/shard_map/ppermute | solution.py:634
  384.4 32.8 %collective-permute-start.37 = (bf16[256,512]{1,0:T(8,128)(2,1)S(1)}, bf16[256,512]{1,0:T(8,128)(2,1)S(1)}, u32[]{:S(2)}, u32[]{:S(2)}) collective-permute-start(bf16[256,512]{1,0:T(8,128)(2,1)S(1)} %fusion.52), channel_id=1, source_target_pairs={{0,2},{1,3},{2,0},{3,1},{4,6},{5,7},{6,4},{7,5},{8,10},{9,11},{10,... | collective-permute-start | bytes 786440 | tf_op jit(solution)/shard_map/ppermute | solution.py:634
  385.6 31.6 %collective-permute-start.38 = (bf16[256,512]{1,0:T(8,128)(2,1)S(1)}, bf16[256,512]{1,0:T(8,128)(2,1)S(1)}, u32[]{:S(2)}, u32[]{:S(2)}) collective-permute-start(bf16[256,512]{1,0:T(8,128)(2,1)S(1)} %fusion.51), channel_id=1, source_target_pairs={{0,4},{1,5},{2,6},{3,7},{4,0},{5,1},{6,2},{7,3},{8,12},{9,13},{10,... | collective-permute-start | bytes 786440 | tf_op jit(solution)/shard_map/ppermute | solution.py:634
  425.4 26.9 %collective-permute-start.40 = (bf16[512,4096]{1,0:T(8,128)(2,1)}, bf16[512,4096]{1,0:T(8,128)(2,1)}, u32[]{:S(2)}, u32[]{:S(2)}) collective-permute-start(bf16[512,4096]{1,0:T(8,128)(2,1)} %convolution_convert_fusion.1), channel_id=1, source_target_pairs={{0,1},{1,0},{2,3},{3,2},{4,5},{5,4},{6,7},{7,6},{8,9},{9,8},{10,11... | collective-permute-start | bytes 12582920 | tf_op jit(solution)/shard_map/ppermute | solution.py:634
  436.6 24.7 %collective-permute-start.41 = (bf16[88,1024]{1,0:T(8,128)(2,1)S(1)}, bf16[88,1024]{1,0:T(8,128)(2,1)S(1)}, u32[]{:S(2)}, u32[]{:S(2)}) collective-permute-start(bf16[88,1024]{1,0:T(8,128)(2,1)S(1)} %get-tuple-element.353), channel_id=1, source_target_pairs={{0,8},{1,9},{2,10},{3,11},{4,12},{5,13},{6,14},{7,15},{8,16},{9,17... | collective-permute-start | bytes 540680 | tf_op jit(solution)/shard_map/ppermute | solution.py:738
  439.2 22.1 %collective-permute-start.42 = (bf16[88,1024]{1,0:T(8,128)(2,1)S(1)}, bf16[88,1024]{1,0:T(8,128)(2,1)S(1)}, u32[]{:S(2)}, u32[]{:S(2)}) collective-permute-start(bf16[88,1024]{1,0:T(8,128)(2,1)S(1)} %get-tuple-element.352), channel_id=1, source_target_pairs={{0,16},{1,17},{2,18},{3,19},{4,20},{5,21},{6,22},{7,23},{8,24},{9,... | collective-permute-start | bytes 540680 | tf_op jit(solution)/shard_map/ppermute | solution.py:738
  440.6 20.8 %collective-permute-start.43 = (bf16[88,1024]{1,0:T(8,128)(2,1)S(1)}, bf16[88,1024]{1,0:T(8,128)(2,1)S(1)}, u32[]{:S(2)}, u32[]{:S(2)}) collective-permute-start(bf16[88,1024]{1,0:T(8,128)(2,1)S(1)} %get-tuple-element.351), channel_id=1, source_target_pairs={{0,24},{1,25},{2,26},{3,27},{4,28},{5,29},{6,30},{7,31},{8,0},{9,1... | collective-permute-start | bytes 540680 | tf_op jit(solution)/shard_map/ppermute | solution.py:738
  462.0 27.7 %collective-permute-start.44 = (bf16[256,2048]{1,0:T(8,128)(2,1)}, bf16[256,2048]{1,0:T(8,128)(2,1)S(1)}, u32[]{:S(2)}, u32[]{:S(2)}) collective-permute-start(bf16[256,2048]{1,0:T(8,128)(2,1)} %fusion.16), channel_id=1, source_target_pairs={{0,2},{1,3},{2,0},{3,1},{4,6},{5,7},{6,4},{7,5},{8,10},{9,11},{10,... | collective-permute-start | bytes 3145736 | tf_op jit(solution)/shard_map/ppermute | solution.py:634
  462.2 27.6 %collective-permute-start.45 = (bf16[256,2048]{1,0:T(8,128)(2,1)}, bf16[256,2048]{1,0:T(8,128)(2,1)S(1)}, u32[]{:S(2)}, u32[]{:S(2)}) collective-permute-start(bf16[256,2048]{1,0:T(8,128)(2,1)} %fusion.17), channel_id=1, source_target_pairs={{0,4},{1,5},{2,6},{3,7},{4,0},{5,1},{6,2},{7,3},{8,12},{9,13},{10,... | collective-permute-start | bytes 3145736 | tf_op jit(solution)/shard_map/ppermute | solution.py:634
  470.4 19.3 %collective-permute-start.46 = (bf16[128,512]{1,0:T(8,128)(2,1)S(1)}, bf16[128,512]{1,0:T(8,128)(2,1)S(1)}, u32[]{:S(2)}, u32[]{:S(2)}) collective-permute-start(bf16[128,512]{1,0:T(8,128)(2,1)S(1)} %copy-done.69), channel_id=1, source_target_pairs={{0,4},{1,5},{2,6},{3,7},{4,0},{5,1},{6,2},{7,3},{8,12},{9,13},{10,... | collective-permute-start | bytes 393224 | tf_op jit(solution)/shard_map/ppermute | solution.py:634
  517.1 30.0 %collective-permute-start.57 = (bf16[32,5120]{1,0:T(8,128)(2,1)S(1)}, bf16[32,5120]{1,0:T(8,128)(2,1)S(1)}, u32[]{:S(2)}, u32[]{:S(2)}) collective-permute-start(bf16[32,5120]{1,0:T(8,128)(2,1)S(1)} %get-tuple-element.338), channel_id=1, source_target_pairs={{0,16},{1,17},{2,18},{3,19},{4,20},{5,21},{6,22},{7,23},{8,24},{9,... | collective-permute-start | bytes 983048 | tf_op jit(solution)/shard_map/ppermute | solution.py:738
  521.3 25.8 %collective-permute-start.56 = (bf16[32,5120]{1,0:T(8,128)(2,1)S(1)}, bf16[32,5120]{1,0:T(8,128)(2,1)S(1)}, u32[]{:S(2)}, u32[]{:S(2)}) collective-permute-start(bf16[32,5120]{1,0:T(8,128)(2,1)S(1)} %get-tuple-element.336), channel_id=1, source_target_pairs={{0,8},{1,9},{2,10},{3,11},{4,12},{5,13},{6,14},{7,15},{8,16},{9,17... | collective-permute-start | bytes 983048 | tf_op jit(solution)/shard_map/ppermute | solution.py:738
  (118 other events, 984.5 us)
Sparse Core Ops, SparseCore 0:
  11.5 88.7 all-gather.2
  103.2 107.5 all-gather.4
  256.7 206.9 reduce-scatter.1
